TPU v7x, 32 devices: a whole 2x2x4 slice. The times are simulated.
32 devices in a mesh: seq: 2 (over x), mp: 16 (over z, y, core).
Axes of the slice: x: 2, y: 2, z: 4, core: 2. Of those that a mesh axis runs over, the one named last changes fastest.
Arguments:
- tokens: bfloat16 [512, 4, 1536], P('seq'), may hold values from -6 to 6
- target: bfloat16 [512, 4, 1536], P(('seq', 'mp')), may hold values from -6 to 6
- lengths: int32 [4], replicated, may hold values from 128 to 512, as said below
- routes: int32 [512, 4, 6], P(('seq', 'mp')), may hold values from 0 to 15, all different within a row; in each aligned block of 64 rows (0 to 63, 64 to 127, ..., all dimensions but the last counted through in order) at most 48 rows name the same one
- route_weight: float32 [512, 4, 6], P(('seq', 'mp')), may hold values from 0.1 to 0.4
- in_gain: bfloat16 [1536], P(('seq', 'mp')), may hold values from 0.5 to 1.5
- gate_proj: bfloat16 [1536, 3072], P(None, 'mp'), may hold values from -0.15625 to 0.15625
- value_proj: bfloat16 [1536, 3072], P(None, 'mp'), may hold values from -0.15625 to 0.15625
- state_proj: bfloat16 [1536, 256], P(('seq', 'mp')), may hold values from -0.078125 to 0.078125
- step_proj: bfloat16 [1536, 48], P(None, 'mp'), may hold values from -0.15625 to 0.15625
- conv_value: float32 [4, 3072], P(None, 'mp'), may hold values from -3 to 3
- conv_value_bias: float32 [3072], P('mp'), may hold values from -3 to 3
- conv_state: bfloat16 [256, 4], P(('seq', 'mp')), may hold values from -3 to 3
- conv_state_bias: bfloat16 [256], P(('seq', 'mp')), may hold values from -3 to 3
- step_bias: float32 [48], P('mp'), may hold values from -4 to -1
- decay_log: float32 [48], P('mp'), may hold values from -8 to -1
- skip_gain: float32 [48], P('mp'), may hold values from 0.5 to 2
- mixer_gain: float32 [3072], P('mp'), may hold values from 0.5 to 1.5
- out_proj: bfloat16 [3072, 1536], P('mp'), may hold values from -0.109375 to 0.109375
- ffn_gain: bfloat16 [1536], P(('seq', 'mp')), may hold values from 0.5 to 1.5
- shared_gate: bfloat16 [1536, 1024], P(('seq', 'mp')), may hold values from -0.15625 to 0.15625
- shared_up: bfloat16 [1536, 1024], P(('seq', 'mp')), may hold values from -0.15625 to 0.15625
- shared_down: bfloat16 [1024, 1536], P(('seq', 'mp')), may hold values from -0.1875 to 0.1875
- expert_gate: bfloat16 [16, 1536, 512], P('mp'), may hold values from -0.15625 to 0.15625
- routed_up_weights: bfloat16 [16, 1536, 512], P('mp'), may hold values from -0.15625 to 0.15625
- expert_down: bfloat16 [16, 512, 1536], P('mp'), may hold values from -0.25 to 0.25
Outputs:
- block_out: bfloat16 [512, 4, 1536], P(('seq', 'mp'))
- tokens_grad: float32 [512, 4, 1536], P(('seq', 'mp'))
- in_gain_grad: float32 [1536], P(('seq', 'mp'))
- gate_proj_grad: float32 [1536, 3072], P(None, 'mp')
- value_proj_grad: float32 [1536, 3072], P(None, 'mp')
- state_proj_grad: float32 [1536, 256], P(('seq', 'mp'))
- step_proj_grad: float32 [1536, 48], P(None, 'mp')
- conv_value_grad: float32 [4, 3072], P(None, 'mp')
- conv_value_bias_grad: float32 [3072], P('mp')
- conv_state_grad: float32 [256, 4], P(('seq', 'mp'))
- conv_state_bias_grad: float32 [256], P(('seq', 'mp'))
- step_bias_grad: float32 [48], P('mp')
- decay_log_grad: float32 [48], P('mp')
- skip_gain_grad: float32 [48], P('mp')
- mixer_gain_grad: float32 [3072], P('mp')
- out_proj_grad: float32 [3072, 1536], P('mp')
- ffn_gain_grad: float32 [1536], P(('seq', 'mp'))
- shared_gate_grad: float32 [1536, 1024], P(('seq', 'mp'))
- shared_up_grad: float32 [1536, 1024], P(('seq', 'mp'))
- shared_down_grad: float32 [1024, 1536], P(('seq', 'mp'))
- expert_gate_grad: float32 [16, 1536, 512], P('mp')
- expert_up_grad: float32 [16, 1536, 512], P('mp')
- expert_down_grad: float32 [16, 512, 1536], P('mp')
Inputs may be any that keep to these rules, and one draw needn't show every extreme that they name: `routes`: each row names 6 different experts. In each aligned block of 64 rows (the rows of one device), no expert is named by more than 48 rows, a bound that some block reaches. `lengths`: some sequence has all 512 slots true.
All inputs are finite; a program needn't handle non-finite values.
Results may differ from a plain program's by a relative error of at most 0.018.
The roundings to bfloat16 on the way count: a program that leaves them out, or rounds other values in their place, can miss the bound.
Values may be sent and summed in bfloat16 or wider, within the bound.
No kernel may reach another device: no remote copies, remote signals or barrier semaphores. Data moves between devices by JAX's collectives and lax.ppermute only.
A program may use at most 192 MiB of HBM per device.

v0:
```python
import jax
import jax.numpy as jnp
from jax import lax
from jax.sharding import PartitionSpec as P

STATE = 128
INNER = 3072


epsilon = 1e-05
highest = lax.Precision.HIGHEST


def shifted(block, axis, distance):
    devices = range(lax.axis_size(axis))
    route = [(i - distance, i) for i in devices if i - distance in devices]
    return lax.ppermute(block, axis, route)


def entering_2(value, axis, join, neutral, backward):
    count, mine = (lax.axis_size(axis), lax.axis_index(axis))
    pieces = jax.tree.map(lambda part: lax.all_gather(part, axis), value)
    if backward:
        pieces = jax.tree.map(lambda part: part[::-1], pieces)
        mine = count - 1 - mine
    running = jax.tree.map(
        lambda part, zero: jnp.full_like(part, 0) + jnp.asarray(zero, part.dtype), value, neutral
    )

    def hop(position, running):
        longer = join(running, jax.tree.map(lambda part: part[position], pieces))
        return jax.tree.map(lambda new, old: jnp.where(position < mine, new, old), longer, running)

    return lax.fori_loop(0, count - 1, hop, running)


def rms_scale(values, gain):
    return values * lax.rsqrt(jnp.mean(values * values, axis=-1, keepdims=True) + epsilon) * gain


def silu_slope(values):
    sigmoid_val = jax.nn.sigmoid(values)
    return sigmoid_val * (1.0 + values * (1.0 - sigmoid_val))


def conv_decay(
    extended, conv_weight, conv_bias, step_raw, step_bias, decay_log, inner_width, state_width
):
    length = step_raw.shape[0]
    preact = conv_bias + conv_weight[0] * extended[0:length]
    for offset in range(1, conv_weight.shape[0]):
        preact = preact + conv_weight[offset] * extended[offset : offset + length]
    activated = jax.nn.silu(preact)
    head_count = step_raw.shape[-1]
    values = activated[..., :inner_width].reshape(
        length, activated.shape[1], head_count, inner_width // head_count
    )
    input_matrix_b = activated[..., inner_width : inner_width + state_width]
    c_matrix = activated[..., inner_width + state_width :]
    step_size = jax.nn.softplus(step_raw + step_bias)
    log_decay = -jnp.exp(decay_log) * step_size
    return (values, input_matrix_b, c_matrix, step_size, log_decay)


def ssd_output(values, input_matrix_b, c_matrix, step_size, log_decay, entering, skip_gain):
    cumulative = jnp.cumsum(log_decay, axis=0)
    length = cumulative.shape[0]
    causal = (jnp.arange(length)[:, None] >= jnp.arange(length)[None, :])[:, :, None, None]
    log_gap = jnp.where(causal, cumulative[:, None] - cumulative[None, :], 0.0)
    decay_mask = jnp.where(causal, jnp.exp(log_gap), 0.0)
    intersection = jnp.einsum("tbn,sbn->tsb", c_matrix, input_matrix_b, precision=highest)
    weighted = decay_mask * intersection[..., None]
    scaled = values * step_size[..., None]
    within = jnp.einsum("tsbh,sbhp->tbhp", weighted, scaled, precision=highest)
    carried = jnp.exp(cumulative)[..., None] * jnp.einsum(
        "tbn,bhpn->tbhp", c_matrix, entering, precision=highest
    )
    return within + carried + skip_gain[:, None] * values


def state_update(values, input_matrix_b, step_size, log_decay):
    cumulative = jnp.cumsum(log_decay, axis=0)
    decay_total = jnp.exp(cumulative[-1])
    tail_weight = jnp.exp(cumulative[-1] - cumulative) * step_size
    local_state = jnp.einsum(
        "sbh,sbhp,sbn->bhpn", tail_weight, values, input_matrix_b, precision=highest
    )
    return (decay_total, local_state)


def chain_combine(earlier, latter):
    return (earlier[0] * latter[0], latter[0][..., None, None] * earlier[1] + latter[1])


def gather_shared(
    in_gain, state_proj, conv_state, conv_state_bias, ffn_gain, shared_gate, shared_up, shared_down
):
    return (
        lax.all_gather(in_gain, ("seq", "mp"), axis=0, tiled=True),
        lax.all_gather(state_proj, ("seq", "mp"), axis=0, tiled=True),
        lax.all_gather(conv_state, ("seq", "mp"), axis=0, tiled=True),
        lax.all_gather(conv_state_bias, ("seq", "mp"), axis=0, tiled=True),
        lax.all_gather(ffn_gain, ("seq", "mp"), axis=0, tiled=True),
        lax.all_gather(shared_gate, ("seq", "mp"), axis=0, tiled=True),
        lax.all_gather(shared_up, ("seq", "mp"), axis=0, tiled=True),
        lax.all_gather(shared_down, ("seq", "mp"), axis=0, tiled=True),
    )


def body(
    tokens,
    target,
    lengths,
    routes,
    route_weight,
    in_gain,
    gate_proj,
    value_proj,
    state_proj,
    step_proj,
    conv_value,
    conv_value_bias,
    conv_state,
    conv_state_bias,
    step_bias,
    decay_log,
    skip_gain,
    mixer_gain,
    out_proj,
    ffn_gain,
    shared_gate,
    shared_up,
    shared_down,
    expert_gate,
    routed_up_weights,
    expert_down,
):
    mp_count = lax.axis_size("mp")
    slot_count, seq_count, model_width = tokens.shape
    shared_expert_rows = slot_count // mp_count
    inner_width = gate_proj.shape[1]
    route_count = routes.shape[-1]
    local_experts = expert_gate.shape[0]
    expert_count = local_experts * mp_count
    row_count = shared_expert_rows * seq_count
    capacity = min(row_count, 2 * row_count * route_count // expert_count)
    window = conv_value.shape[0]
    gathered = gather_shared(
        in_gain,
        state_proj,
        conv_state,
        conv_state_bias,
        ffn_gain,
        shared_gate,
        shared_up,
        shared_down,
    )
    (
        gain_first,
        state_whole,
        conv_state_whole,
        conv_bias_whole,
        gain_second,
        gate_complete,
        up_whole,
        down_whole,
    ) = gathered
    inputs = tokens.astype(jnp.float32)
    normed = rms_scale(inputs, gain_first.astype(jnp.float32)).astype(jnp.bfloat16)
    gate_raw = jnp.dot(normed, gate_proj, preferred_element_type=jnp.float32)
    value_raw = jnp.dot(normed, value_proj, preferred_element_type=jnp.float32)
    state_raw = jnp.dot(normed, state_whole, preferred_element_type=jnp.float32)
    step_raw = jnp.dot(normed, step_proj, preferred_element_type=jnp.float32)
    conv_input = jnp.concatenate([value_raw, state_raw], axis=-1)
    edge_rows = shifted(conv_input[slot_count - window + 1 :], "seq", 1)
    extended = jnp.concatenate([edge_rows, conv_input], axis=0)
    conv_weight = jnp.concatenate([conv_value, conv_state_whole.astype(jnp.float32).T], axis=1)
    conv_bias = jnp.concatenate([conv_value_bias, conv_bias_whole.astype(jnp.float32)])

    def first_piece(ext_values, weight_values, bias_values, step_values, bias_step, decay_values):
        return conv_decay(
            ext_values,
            weight_values,
            bias_values,
            step_values,
            bias_step,
            decay_values,
            inner_width,
            STATE,
        )

    mixer_inputs, first_back = jax.vjp(
        first_piece, extended, conv_weight, conv_bias, step_raw, step_bias, decay_log
    )
    values, input_matrix_b, c_matrix, step_size, log_decay = mixer_inputs
    local_out, state_back = jax.vjp(state_update, values, input_matrix_b, step_size, log_decay)
    decay_total, local_state = local_out
    prefix = entering_2(
        (decay_total, local_state),
        "seq",
        chain_combine,
        (jnp.ones_like(decay_total), jnp.zeros_like(local_state)),
        False,
    )
    entering = prefix[1]

    def second_piece(
        in_values,
        in_bmatrix,
        in_cmatrix,
        in_step,
        in_decay,
        in_state,
        in_skip,
        in_gate,
        in_gain_mix,
    ):
        result = ssd_output(in_values, in_bmatrix, in_cmatrix, in_step, in_decay, in_state, in_skip)
        gated_part = result.reshape(in_gate.shape) * jax.nn.silu(in_gate)
        return (gated_part, gated_part * in_gain_mix)

    gated_pair, second_back = jax.vjp(
        second_piece,
        values,
        input_matrix_b,
        c_matrix,
        step_size,
        log_decay,
        entering,
        skip_gain,
        gate_raw,
        mixer_gain,
    )
    gated_out, scaled = gated_pair
    scaled_low = scaled.astype(jnp.bfloat16)
    mix_part = jnp.dot(scaled_low, out_proj, preferred_element_type=jnp.float32)
    pre_mix, square_sum = (
        lax.psum_scatter(mix_part, "mp", scatter_dimension=0, tiled=True),
        lax.psum_scatter(
            jnp.sum(gated_out * gated_out, axis=-1), "mp", scatter_dimension=0, tiled=True
        ),
    )
    inv_norm = lax.rsqrt(square_sum / INNER + epsilon)
    start_row = lax.axis_index("mp") * shared_expert_rows
    own_inputs = lax.dynamic_slice_in_dim(inputs, start_row, shared_expert_rows, 0)
    hidden = own_inputs + pre_mix * inv_norm[..., None]
    hidden_rows = hidden.reshape(row_count, model_width)
    ffn_input = rms_scale(hidden_rows, gain_second.astype(jnp.float32)).astype(jnp.bfloat16)
    shared_gate_val = jnp.dot(ffn_input, gate_complete, preferred_element_type=jnp.float32)
    shared_up_val = jnp.dot(ffn_input, up_whole, preferred_element_type=jnp.float32)
    shared_act = (jax.nn.silu(shared_gate_val) * shared_up_val).astype(jnp.bfloat16)
    shared_out = jnp.dot(shared_act, down_whole, preferred_element_type=jnp.float32)
    route_flat = routes.reshape(row_count * route_count)
    onehot = (route_flat[:, None] == jnp.arange(expert_count, dtype=jnp.int32)[None, :]).astype(
        jnp.int32
    )
    slot_rank = jnp.sum((jnp.cumsum(onehot, axis=0) - 1) * onehot, axis=1)
    slot_of = route_flat * capacity + slot_rank
    pair_of = (
        jnp.full((expert_count * capacity,), row_count * route_count, jnp.int32)
        .at[slot_of]
        .set(jnp.arange(row_count * route_count, dtype=jnp.int32))
    )
    padded_rows = jnp.concatenate([ffn_input, jnp.zeros((1, model_width), jnp.bfloat16)], axis=0)
    send_rows = padded_rows[pair_of // route_count].reshape(
        mp_count, local_experts, capacity, model_width
    )
    received_rows = lax.all_to_all(send_rows, "mp", split_axis=0, concat_axis=0, tiled=True)
    gate_activation = jnp.einsum(
        "mecd,edf->mecf", received_rows, expert_gate, preferred_element_type=jnp.float32
    )
    up_val = jnp.einsum(
        "mecd,edf->mecf", received_rows, routed_up_weights, preferred_element_type=jnp.float32
    )
    act_val = (jax.nn.silu(gate_activation) * up_val).astype(jnp.bfloat16)
    result = jnp.einsum(
        "mecf,efd->mecd", act_val, expert_down, preferred_element_type=jnp.float32
    ).astype(jnp.bfloat16)
    returned = lax.all_to_all(result, "mp", split_axis=0, concat_axis=0, tiled=True)
    returned, received_rows, gate_activation, up_val, act_val = (
        returned,
        received_rows,
        gate_activation,
        up_val,
        act_val,
    )
    route_rows = route_weight.reshape(row_count, route_count)
    picked = returned.reshape(expert_count * capacity, model_width)[slot_of].reshape(
        row_count, route_count, model_width
    )
    routed = jnp.sum(route_rows[:, :, None] * picked.astype(jnp.float32), axis=1)
    output = hidden_rows + shared_out + routed
    block_out = output.astype(jnp.bfloat16).reshape(shared_expert_rows, seq_count, model_width)
    position = (
        lax.axis_index("seq") * slot_count
        + start_row
        + jnp.arange(shared_expert_rows, dtype=jnp.int32)
    )
    valid_mask = (position[:, None] < lengths[None, :]).astype(jnp.float32).reshape(row_count, 1)
    grad_out = (output - target.astype(jnp.float32).reshape(row_count, model_width)) * valid_mask
    pair_grads = (
        (route_rows[:, :, None] * grad_out[:, None, :])
        .astype(jnp.bfloat16)
        .reshape(row_count * route_count, model_width)
    )
    pair_padded = jnp.concatenate([pair_grads, jnp.zeros((1, model_width), jnp.bfloat16)], axis=0)
    grad_send = pair_padded[pair_of].reshape(mp_count, local_experts, capacity, model_width)
    grad_arrived = lax.all_to_all(grad_send, "mp", split_axis=0, concat_axis=0, tiled=True)
    activation_gradient = jnp.einsum(
        "mecd,efd->mecf", grad_arrived, expert_down, preferred_element_type=jnp.float32
    )
    expert_down_grad = jnp.einsum(
        "mecf,mecd->efd", act_val, grad_arrived, preferred_element_type=jnp.float32
    )
    egate_grad = (activation_gradient * up_val * silu_slope(gate_activation)).astype(jnp.bfloat16)
    expert_up_gradient = (activation_gradient * jax.nn.silu(gate_activation)).astype(jnp.bfloat16)
    expert_gate_grad = jnp.einsum(
        "lqsb,lqsn->qbn", received_rows, egate_grad, preferred_element_type=jnp.float32
    )
    expert_up_grad = jnp.einsum(
        "lqsb,lqsn->qbn", received_rows, expert_up_gradient, preferred_element_type=jnp.float32
    )
    rows_grad = (
        jnp.einsum("kvsg,vog->kvso", egate_grad, expert_gate, preferred_element_type=jnp.float32)
        + jnp.einsum(
            "kvsg,vog->kvso",
            expert_up_gradient,
            routed_up_weights,
            preferred_element_type=jnp.float32,
        )
    ).astype(jnp.bfloat16)
    returned_grad = lax.all_to_all(rows_grad, "mp", split_axis=0, concat_axis=0, tiled=True)
    routed_grad = jnp.sum(
        returned_grad.reshape(expert_count * capacity, model_width)[slot_of]
        .reshape(row_count, route_count, model_width)
        .astype(jnp.float32),
        axis=1,
    )
    weights_back = gather_shared(
        in_gain,
        state_proj,
        conv_state,
        conv_state_bias,
        ffn_gain,
        shared_gate,
        shared_up,
        shared_down,
    )
    (
        gain_first_back,
        state_whole_back,
        _,
        _,
        gain_second_back,
        gate_whole_back,
        up_whole_back,
        down_whole_back,
    ) = weights_back
    out_grad_low = grad_out.astype(jnp.bfloat16)
    shared_down_grad = jnp.einsum(
        "rf,rd->fd", shared_act, out_grad_low, preferred_element_type=jnp.float32
    )
    shact_grad = jnp.einsum(
        "rd,fd->rf", out_grad_low, down_whole_back, preferred_element_type=jnp.float32
    )
    sgate_grad = (shact_grad * shared_up_val * silu_slope(shared_gate_val)).astype(jnp.bfloat16)
    sup_grad = (shact_grad * jax.nn.silu(shared_gate_val)).astype(jnp.bfloat16)
    shared_gate_grad = jnp.einsum(
        "rd,rf->df", ffn_input, sgate_grad, preferred_element_type=jnp.float32
    )
    shared_up_grad = jnp.einsum(
        "rd,rf->df", ffn_input, sup_grad, preferred_element_type=jnp.float32
    )
    ffn_input_grad = (
        routed_grad
        + jnp.einsum("rf,df->rd", sgate_grad, gate_whole_back, preferred_element_type=jnp.float32)
        + jnp.einsum("rf,df->rd", sup_grad, up_whole_back, preferred_element_type=jnp.float32)
    )
    _, second_norm_back = jax.vjp(rms_scale, hidden_rows, gain_second_back.astype(jnp.float32))
    hidden_part, ffn_gain_grad = second_norm_back(ffn_input_grad)
    hidden_grad_share = (grad_out + hidden_part).reshape(shared_expert_rows, seq_count, model_width)
    mix_grad_low = (hidden_grad_share * inv_norm[..., None]).astype(jnp.bfloat16)
    sum_grad_share = (
        jnp.sum(hidden_grad_share * pre_mix, axis=-1)
        * -0.5
        * inv_norm
        * inv_norm
        * inv_norm
        / INNER
    )
    mix_grad_wide, sum_grad = (
        lax.all_gather(mix_grad_low.astype(jnp.float32), "mp", axis=0, tiled=True),
        lax.all_gather(sum_grad_share, "mp", axis=0, tiled=True),
    )
    mix_grad_all = mix_grad_wide.astype(jnp.bfloat16)
    out_proj_grad = jnp.einsum(
        "sbc,sbd->cd", scaled_low, mix_grad_all, preferred_element_type=jnp.float32
    )
    scaled_grad = jnp.einsum(
        "sbd,cd->sbc", mix_grad_all, out_proj, preferred_element_type=jnp.float32
    )
    gated_grad = 2.0 * gated_out * sum_grad[..., None]
    (
        out_values_grad,
        out_bmatrix_grad,
        out_cmatrix_grad,
        out_step_grad,
        out_decay_grad,
        entering_grad,
        skip_gain_grad,
        gate_raw_grad,
        mixer_gain_grad,
    ) = second_back((gated_grad, scaled_grad))
    suffix = entering_2(
        (decay_total, entering_grad),
        "seq",
        chain_combine,
        (jnp.ones_like(decay_total), jnp.zeros_like(entering_grad)),
        True,
    )
    exit_grad = suffix[1]
    total_grad = jnp.sum(entering * exit_grad, axis=(-2, -1))
    tail_values_grad, tail_bmatrix_grad, tail_step_grad, tail_decay_grad = state_back(
        (total_grad, exit_grad)
    )
    ext_grad, conv_weight_grad, conv_bias_grad, step_raw_grad, step_bias_grad, decay_log_grad = (
        first_back(
            (
                out_values_grad + tail_values_grad,
                out_bmatrix_grad + tail_bmatrix_grad,
                out_cmatrix_grad,
                out_step_grad + tail_step_grad,
                out_decay_grad + tail_decay_grad,
            )
        )
    )
    edge_grad = shifted(ext_grad[: window - 1], "seq", -1)
    conv_grad = ext_grad[window - 1 :] + jnp.concatenate(
        [jnp.zeros((slot_count - window + 1,) + ext_grad.shape[1:], jnp.float32), edge_grad], axis=0
    )
    conv_grad_low = conv_grad.astype(jnp.bfloat16)
    value_grad = conv_grad_low[..., :inner_width]
    state_grad = conv_grad_low[..., inner_width:]
    gate_grad = gate_raw_grad.astype(jnp.bfloat16)
    step_grad = step_raw_grad.astype(jnp.bfloat16)
    partial_value = jnp.einsum(
        "sbc,dc->sbd", gate_grad, gate_proj, preferred_element_type=jnp.float32
    )
    partial_value = partial_value + jnp.einsum(
        "sbc,dc->sbd", value_grad, value_proj, preferred_element_type=jnp.float32
    )
    partial_value = partial_value + jnp.einsum(
        "sbc,dc->sbd", state_grad, state_whole_back, preferred_element_type=jnp.float32
    )
    partial_value = partial_value + jnp.einsum(
        "sbh,dh->sbd", step_grad, step_proj, preferred_element_type=jnp.float32
    )
    normed_grad = lax.psum_scatter(partial_value, "mp", scatter_dimension=0, tiled=True)
    gate_proj_grad = jnp.einsum(
        "sbd,sbc->dc", normed, gate_grad, preferred_element_type=jnp.float32
    )
    value_proj_grad = jnp.einsum(
        "sbd,sbc->dc", normed, value_grad, preferred_element_type=jnp.float32
    )
    state_proj_grad = jnp.einsum(
        "sbd,sbc->dc", normed, state_grad, preferred_element_type=jnp.float32
    )
    step_proj_grad = jnp.einsum(
        "sbd,sbh->dh", normed, step_grad, preferred_element_type=jnp.float32
    )
    _, first_norm_back = jax.vjp(rms_scale, own_inputs, gain_first_back.astype(jnp.float32))
    input_part, in_gain_grad = first_norm_back(normed_grad)
    tokens_grad = input_part + hidden_grad_share
    conv_value_grad = conv_weight_grad[:, :inner_width]
    conv_state_grad = conv_weight_grad[:, inner_width:].T
    conv_value_bias_grad = conv_bias_grad[:inner_width]
    conv_state_bias_grad = conv_bias_grad[inner_width:]
    summed = lax.psum(
        (
            gate_proj_grad,
            value_proj_grad,
            step_proj_grad,
            conv_value_grad,
            conv_value_bias_grad,
            step_bias_grad,
            decay_log_grad,
            skip_gain_grad,
            mixer_gain_grad,
            out_proj_grad,
            expert_gate_grad,
            expert_up_grad,
            expert_down_grad,
        ),
        "seq",
    )
    scattered = (
        lax.psum_scatter(in_gain_grad, ("seq", "mp"), scatter_dimension=0, tiled=True),
        lax.psum_scatter(state_proj_grad, ("seq", "mp"), scatter_dimension=0, tiled=True),
        lax.psum_scatter(conv_state_grad, ("seq", "mp"), scatter_dimension=0, tiled=True),
        lax.psum_scatter(conv_state_bias_grad, ("seq", "mp"), scatter_dimension=0, tiled=True),
        lax.psum_scatter(ffn_gain_grad, ("seq", "mp"), scatter_dimension=0, tiled=True),
        lax.psum_scatter(shared_gate_grad, ("seq", "mp"), scatter_dimension=0, tiled=True),
        lax.psum_scatter(shared_up_grad, ("seq", "mp"), scatter_dimension=0, tiled=True),
        lax.psum_scatter(shared_down_grad, ("seq", "mp"), scatter_dimension=0, tiled=True),
    )
    return (
        block_out,
        tokens_grad,
        scattered[0],
        summed[0],
        summed[1],
        scattered[1],
        summed[2],
        summed[3],
        summed[4],
        scattered[2],
        scattered[3],
        summed[5],
        summed[6],
        summed[7],
        summed[8],
        summed[9],
        scattered[4],
        scattered[5],
        scattered[6],
        scattered[7],
        summed[10],
        summed[11],
        summed[12],
    )


def solution(mesh):
    placed = (
        P("seq", None, None),
        P(("seq", "mp"), None, None),
        P(),
        P(("seq", "mp"), None, None),
        P(("seq", "mp"), None, None),
        P(("seq", "mp")),
        P(None, "mp"),
        P(None, "mp"),
        P(("seq", "mp"), None),
        P(None, "mp"),
        P(None, "mp"),
        P("mp"),
        P(("seq", "mp"), None),
        P(("seq", "mp")),
        P("mp"),
        P("mp"),
        P("mp"),
        P("mp"),
        P("mp", None),
        P(("seq", "mp")),
        P(("seq", "mp"), None),
        P(("seq", "mp"), None),
        P(("seq", "mp"), None),
        P("mp", None, None),
        P("mp", None, None),
        P("mp", None, None),
    )
    return jax.shard_map(
        body,
        mesh=mesh,
        in_specs=placed,
        out_specs=(
            P(("seq", "mp"), None, None),
            P(("seq", "mp"), None, None),
            P(("seq", "mp")),
            P(None, "mp"),
            P(None, "mp"),
            P(("seq", "mp"), None),
            P(None, "mp"),
            P(None, "mp"),
            P("mp"),
            P(("seq", "mp"), None),
            P(("seq", "mp")),
            P("mp"),
            P("mp"),
            P("mp"),
            P("mp"),
            P("mp", None),
            P(("seq", "mp")),
            P(("seq", "mp"), None),
            P(("seq", "mp"), None),
            P(("seq", "mp"), None),
            P("mp", None, None),
            P("mp", None, None),
            P("mp", None, None),
        ),
        check_vma=False,
    )
```

profile of v0, /device:TPU:0, one launch (start us, length us, event | category | flops | bytes accessed | tf_op | source)
XLA Modules:
  0.0 1483.6 jit_solution(1309344460942513882)
XLA Ops:
  10.8 42.1 %all-reduce.26 = (bf16[1536]{0:T(1024)(128)(2,1)S(1)}, bf16[256]{0:T(256)(128)(2,1)S(1)}, bf16[1536]{0:T(1024)(128)(2,1)}) all-reduce(bf16[1536]{0:T(1024)(128)(2,1)S(1)} %dynamic-update-slice.1, bf16[256]{0:T(256)(128)(2,1)S(1)} %dynamic-update-slice, ...), channel_id=1, replica_groups=mesh['seq'=2,'mp'=16] {'seq','mp'}, use_global_device_ids=true, to_apply=%add.17 | all-reduce | flops 3328 | bytes 13312
  55.9 42.6 %all_gather.57 = bf16[1536,256]{1,0:T(8,128)(2,1)S(1)} all-gather(bf16[48,256]{1,0:T(8,128)(2,1)S(1)} %copy-done.98), channel_id=1, replica_groups=mesh['seq'=2,'mp'=16] {'seq','mp'}, dimensions={0}, use_global_device_ids=true | all-gather | bytes 811008 | tf_op jit(solution)/shard_map/all_gather | solution.py:100
  104.6 4.0 collective-permute-start
  109.8 36.4 %all-gather.2 = bf16[32,8,4]{1,2,0:T(4,128)(2,1)S(1)} all-gather(bf16[1,8,4]{1,2,0:T(4,128)(2,1)S(1)} %bitcast.432), channel_id=1, replica_groups=mesh['seq'=2,'mp'=16] {'seq','mp'}, dimensions={0}, use_global_device_ids=true | all-gather | bytes 2112 | tf_op jit(solution)/shard_map/all_gather | solution.py:101
  155.2 4.4 all_gather.58
  167.2 4.4 fusion.27
  174.6 11.2 all-gather
  190.2 5.8 fusion.66
  200.6 4.5 fusion.98
  211.2 5.5 copy_convert_fusion
  216.7 38.8 %reduce-scatter.23.cloned.1.call-done = f32[16,4]{1,0:T(8,128)} async-done(((f32[256,4]{1,0:T(8,128)}), f32[16,4]{1,0:T(8,128)}) %reduce-scatter.23.cloned.1.call-update) | async-done | bytes 272
  256.3 97.8 %reduce-scatter.11.cloned.1.call-done = f32[16,4,1536]{2,0,1:T(8,128)} async-done(((f32[256,4,1536]{2,0,1:T(8,128)}), f32[16,4,1536]{2,0,1:T(8,128)}) %reduce-scatter.11.cloned.1.call-update) | async-done | bytes 393232 | tf_op jit(solution)/shard_map/reduce_scatter | solution.py:238
  356.9 3.8 gather_fusion
  360.7 4.5 all-to-all-start
  365.8 47.1 %all-to-all-done = bf16[16,1,48,1536]{3,2,1,0:T(8,128)(2,1)} async-done(((bf16[16,1,48,1536]{3,2,1,0:T(8,128)(2,1)}), bf16[16,1,48,1536]{3,2,1,0:T(8,128)(2,1)}, u32[]{:S(2)}, u32[]{:S(2)}) %all-to-all-start) | async-done | bytes 2359328 | tf_op jit(solution)/shard_map/all_to_all | solution.py:268
  425.0 16.6 %all-to-all-start.1 = ((bf16[16,1,48,1536]{3,2,1,0:T(8,128)(2,1)}), bf16[16,1,48,1536]{3,2,1,0:T(8,128)(2,1)}, u32[]{:S(2)}, u32[]{:S(2)}) async-start(bf16[16,1,48,1536]{3,2,1,0:T(8,128)(2,1)} %fusion.10), calls=%async_computation.2 | async-start | bytes 4718592 | tf_op jit(solution)/shard_map/all_to_all | solution.py:279
  448.9 38.6 %all-to-all-done.1 = bf16[16,1,48,1536]{3,2,1,0:T(8,128)(2,1)} async-done(((bf16[16,1,48,1536]{3,2,1,0:T(8,128)(2,1)}), bf16[16,1,48,1536]{3,2,1,0:T(8,128)(2,1)}, u32[]{:S(2)}, u32[]{:S(2)}) %all-to-all-start.1) | async-done | bytes 2359328 | tf_op jit(solution)/shard_map/all_to_all | solution.py:279
  487.5 6.2 gather_fusion.1
  510.9 3.8 gather_fusion.2
  514.7 66.6 %all_to_all.20 = bf16[16,1,48,1536]{3,2,1,0:T(8,128)(2,1)S(1)} all-to-all(bf16[16,1,48,1536]{3,2,1,0:T(8,128)(2,1)} %bitcast.399), channel_id=1, replica_groups=mesh['seq'=2,'mp'=16] {'mp'}, dimensions={0} | all-to-all | bytes 4718592 | tf_op jit(solution)/shard_map/all_to_all | solution.py:308
  588.1 4.2 all-to-all-start.3
  596.0 41.8 %all-to-all-done.3 = bf16[16,1,48,1536]{3,2,1,0:T(8,128)(2,1)S(1)} async-done(((bf16[16,1,48,1536]{3,2,1,0:T(8,128)(2,1)}), bf16[16,1,48,1536]{3,2,1,0:T(8,128)(2,1)S(1)}, u32[]{:S(2)}, u32[]{:S(2)}) %all-to-all-start.3) | async-done | bytes 2359328 | tf_op jit(solution)/shard_map/all_to_all | solution.py:332
  643.7 3.7 reduce_sum.281
  655.8 28.4 %all-gather.3 = f32[16,16,4]{1,2,0:T(4,128)S(1)} all-gather(f32[1,16,4]{1,2,0:T(4,128)S(1)} %fusion.179), channel_id=1, replica_groups=mesh['seq'=2,'mp'=16] {'mp'}, dimensions={0}, use_global_device_ids=true | all-gather | bytes 4352 | tf_op jit(solution)/shard_map/all_gather | solution.py:393
  684.3 24.6 %all-gather.15.cloned.1.call-done = bf16[256,4,1536]{2,0,1:T(8,128)(2,1)} async-done(((bf16[16,4,1536]{2,0,1:T(8,128)(2,1)}), bf16[256,4,1536]{2,0,1:T(8,128)(2,1)}) %all-gather.15.cloned.1.call-update) | async-done | bytes 3145744 | tf_op jit(solution)/shard_map/all_gather | solution.py:392
  709.0 5.4 multiply_reduce_fusion.8
  716.4 4.8 fusion.23
  724.2 12.1 all-gather.1
  741.8 3.8 multiply_reduce_fusion.10
  746.2 16.3 %reduce-window.34 = f32[3,4,2,128]{3,2,1,0:T(2,128)} reduce-window(f32[3,4,2,128]{3,2,1,0:T(2,128)} %copy.334, f32[]{:T(128)} %constant.56.clone.1), window={size=1x1x1x128 pad=0_0x0_0x0_0x0_127}, to_apply=%region_20.21 | reduce-window | flops 390144 | bytes 24580 | tf_op jit(solution)/shard_map/reduce-window.4
  771.0 16.3 %reduce-window.36 = f32[3,4,2,128]{3,2,1,0:T(2,128)} reduce-window(f32[3,4,2,128]{3,2,1,0:T(2,128)} %copy.340, f32[]{:T(128)} %constant.56.clone.1), window={size=1x1x1x128 pad=0_0x0_0x0_0x0_127}, to_apply=%region_24.25 | reduce-window | flops 390144 | bytes 24580 | tf_op jit(solution)/shard_map/reduce-window.6
  792.9 4.2 multiply_reduce_fusion.4
  803.6 3.7 fusion.170
  807.4 3.8 fusion.100
  811.4 3.8 pad_add_fusion
  820.8 7.0 add_add_fusion
  828.8 3.7 fusion.206
  838.2 3.7 fusion.152
  842.1 5.4 convolution_bitcast_fusion
  850.7 5.0 convolution_bitcast_fusion.1
  855.7 4.9 convolution_bitcast_fusion.2
  875.9 12.1 all-reduce.24
  888.8 23.9 %reduce-scatter.13.cloned.1.call-done = f32[16,4,1536]{2,0,1:T(8,128)} async-done(((f32[256,4,1536]{2,0,1:T(8,128)}), f32[16,4,1536]{2,0,1:T(8,128)}) %reduce-scatter.13.cloned.1.call-update) | async-done | bytes 393232 | tf_op jit(solution)/shard_map/reduce_scatter | solution.py:458
  914.0 41.1 %all-reduce.23 = (f32[1536]{0:T(1024)S(1)}, f32[256,4]{0,1:T(4,128)S(1)}, f32[256]{0:T(256)S(1)}, f32[1536]{0:T(1024)S(1)}) all-reduce(f32[1536]{0:T(1024)S(1)} %get-tuple-element.197, f32[256,4]{0,1:T(4,128)S(1)} %slice_bitcast_fusion, f32[256]{0:T(256)} %slice.123, ...), channel_id=7, replica_groups=mesh['seq'=2,'mp'=16] {'seq','mp'}, use_global_device_ids=true, to_apply=%region_30.31.clone | all-reduce | flops 4352 | bytes 34816
  960.7 124.6 %reduce-scatter.17.cloned.1.call-done = f32[48,1024]{1,0:T(8,128)} async-done(((f32[1536,1024]{1,0:T(8,128)}), f32[48,1024]{1,0:T(8,128)}) %reduce-scatter.17.cloned.1.call-update) | async-done | bytes 196624 | tf_op jit(solution)/shard_map/reduce_scatter | solution.py:502
  1085.3 154.7 %reduce-scatter.19.cloned.1.call-done = f32[48,1024]{1,0:T(8,128)} async-done(((f32[1536,1024]{1,0:T(8,128)}), f32[48,1024]{1,0:T(8,128)}) %reduce-scatter.19.cloned.1.call-update) | async-done | bytes 196624 | tf_op jit(solution)/shard_map/reduce_scatter | solution.py:503
  1240.0 120.2 %reduce-scatter.21.cloned.1.call-done = f32[32,1536]{1,0:T(8,128)} async-done(((f32[1024,1536]{1,0:T(8,128)}), f32[32,1536]{1,0:T(8,128)}) %reduce-scatter.21.cloned.1.call-update) | async-done | bytes 196624 | tf_op jit(solution)/shard_map/reduce_scatter | solution.py:504
  1360.2 102.6 %reduce-scatter.15.cloned.1.call-done = f32[48,256]{1,0:T(8,128)} async-done(((f32[1536,256]{1,0:T(8,128)}), f32[48,256]{1,0:T(8,128)}) %reduce-scatter.15.cloned.1.call-update) | async-done | bytes 49168 | tf_op jit(solution)/shard_map/reduce_scatter | solution.py:498
  (499 shorter events, 195.1 us)
Async XLA Ops:
  8.0 414.2 %copy-start = (bf16[1,512,1536]{2,1,0:T(8,128)(2,1)S(1)}, bf16[1,512,1536]{2,1,0:T(8,128)(2,1)}, u32[]{:S(2)}) copy-start(bf16[1,512,1536]{2,1,0:T(8,128)(2,1)} %param.51) | copy-start | bytes 4718596
  8.0 47.8 %copy-start.98 = (bf16[48,256]{1,0:T(8,128)(2,1)S(1)}, bf16[48,256]{1,0:T(8,128)(2,1)}, u32[]{:S(2)}) copy-start(bf16[48,256]{1,0:T(8,128)(2,1)} %param.34) | copy-start | bytes 73732
  8.1 247.5 %reduce-scatter.23.cloned.1.call-start = ((), (), s32[]{:S(2)}) async-start(), calls=%async_computation.21 | async-start | bytes 139264
  52.9 45.6 %copy-start.16 = (bf16[256,4,1536]{2,1,0:T(4,128)(2,1)S(1)}, bf16[256,4,1536]{2,1,0:T(4,128)(2,1)}, u32[]{:S(2)}) copy-start(bf16[256,4,1536]{2,1,0:T(4,128)(2,1)} %param.26) | copy-start | bytes 9437188
  52.9 93.5 %copy-start.83 = (f32[1536]{0:T(1024)}, f32[1536]{0:T(1024)S(1)}, u32[]{:S(2)}) copy-start(f32[1536]{0:T(1024)S(1)} %convert_element_type.124) | copy-start | bytes 18436
  55.9 90.5 %copy-start.126 = (f32[256,4]{0,1:T(4,128)}, f32[256,4]{0,1:T(4,128)S(1)}, u32[]{:S(2)}) copy-start(f32[256,4]{0,1:T(4,128)S(1)} %add_rsqrt_fusion) | copy-start | bytes 12292
  99.9 65.3 %copy-start.6 = (f32[256,4,256]{0,2,1:T(8,128)}, f32[256,4,256]{0,2,1:T(8,128)S(1)}, u32[]{:S(2)}) copy-start(f32[256,4,256]{0,2,1:T(8,128)S(1)} %fusion.86) | copy-start | bytes 3145732
  101.2 64.0 %copy-start.20 = (f32[256,4,192]{0,2,1:T(8,128)}, f32[256,4,192]{0,2,1:T(8,128)S(1)}, u32[]{:S(2)}) copy-start(f32[256,4,192]{0,2,1:T(8,128)S(1)} %fusion.105) | copy-start | bytes 2359300
  101.2 45.2 %copy-start.114 = (bf16[1536,3]{0,1:T(4,128)(2,1)S(1)}, bf16[1536,3]{0,1:T(4,128)(2,1)}, u32[]{:S(2)}) copy-start(bf16[1536,3]{0,1:T(4,128)(2,1)} %param.35) | copy-start | bytes 27652
  104.6 58.6 %collective-permute-start = (f32[3,4,448]{2,1,0:T(4,128)}, f32[3,4,448]{2,1,0:T(4,128)}, u32[]{:S(2)}, u32[]{:S(2)}) collective-permute-start(f32[3,4,448]{2,1,0:T(4,128)} %copy.289), channel_id=1, source_target_pairs={{0,16},{1,17},{2,18},{3,19},{4,20},{5,21},{6,22},{7,23},{8,24},{9,... | collective-permute-start | bytes 64520 | tf_op jit(solution)/shard_map/ppermute | solution.py:17
  149.3 17.8 %copy-start.79 = (f32[256,4,3]{0,2,1:T(4,128)}, f32[256,4,3]{0,2,1:T(4,128)S(1)}, u32[]{:S(2)}) copy-start(f32[256,4,3]{0,2,1:T(4,128)S(1)} %fusion.172) | copy-start | bytes 36868
  154.4 12.7 copy-start.74
  159.6 28.7 %copy-start.93 = (f32[4,3]{1,0:T(4,128)}, f32[4,3]{1,0:T(4,128)S(1)}, u32[]{:S(2)}) copy-start(f32[4,3]{1,0:T(4,128)S(1)} %get-tuple-element.271) | copy-start | bytes 148
  171.6 16.6 %copy-start.4 = (f32[256,4,448]{0,2,1:T(8,128)}, f32[256,4,448]{0,2,1:T(8,128)S(1)}, u32[]{:S(2)}) copy-start(f32[256,4,448]{0,2,1:T(8,128)S(1)} %get-tuple-element.244) | copy-start | bytes 5505028
  200.5 153.7 %reduce-scatter.11.cloned.1.call-start = ((), (), s32[]{:S(2)}) async-start(), calls=%async_computation.11 | async-start | bytes 6684672 | tf_op jit(solution)/shard_map/reduce_scatter | solution.py:238
  205.1 237.8 %all-gather.9.cloned.1.call-start = ((), (), s32[]{:S(2)}) async-start(), calls=%async_computation.12 | async-start | bytes 3244032 | tf_op jit(solution)/shard_map/all_gather | solution.py:104
  205.6 239.9 %all-gather.11.cloned.1.call-start = ((), (), s32[]{:S(2)}) async-start(), calls=%async_computation.13 | async-start | bytes 3244032 | tf_op jit(solution)/shard_map/all_gather | solution.py:105
  206.7 150.0 %copy-start.81 = (f32[1536]{0:T(1024)}, f32[1536]{0:T(1024)S(1)}, u32[]{:S(2)}) copy-start(f32[1536]{0:T(1024)S(1)} %convert_element_type.127) | copy-start | bytes 18436
  256.3 99.7 %copy-start.102 = (f32[16,4]{0,1:T(4,128)}, f32[16,4]{0,1:T(4,128)S(1)}, u32[]{:S(2)}) copy-start(f32[16,4]{0,1:T(4,128)S(1)} %copy.380) | copy-start | bytes 772
  256.3 99.7 %copy-start.99 = (f32[16,4]{0,1:T(4,128)}, f32[16,4]{0,1:T(4,128)S(1)}, u32[]{:S(2)}) copy-start(f32[16,4]{0,1:T(4,128)S(1)} %add_rsqrt_fusion.1) | copy-start | bytes 772
  356.5 143.4 %copy-start.26 = (f32[64,1536]{1,0:T(8,128)}, f32[64,1536]{1,0:T(8,128)S(1)}, u32[]{:S(2)}) copy-start(f32[64,1536]{1,0:T(8,128)S(1)} %reshape.399) | copy-start | bytes 1179652
  356.8 88.8 %copy-start.22 = (bf16[64,1536]{1,0:T(8,128)(2,1)}, bf16[64,1536]{1,0:T(8,128)(2,1)S(1)}, u32[]{:S(2)}) copy-start(bf16[64,1536]{1,0:T(8,128)(2,1)S(1)} %multiply_convert_fusion.4) | copy-start | bytes 589828
  360.7 52.2 %all-to-all-start = ((bf16[16,1,48,1536]{3,2,1,0:T(8,128)(2,1)}), bf16[16,1,48,1536]{3,2,1,0:T(8,128)(2,1)}, u32[]{:S(2)}, u32[]{:S(2)}) async-start(bf16[16,1,48,1536]{3,2,1,0:T(8,128)(2,1)} %bitcast.398), calls=%async_computation.1 | async-start | bytes 4718592 | tf_op jit(solution)/shard_map/all_to_all | solution.py:268
  365.2 134.7 %all-gather.13.cloned.1.call-start = ((), (), s32[]{:S(2)}) async-start(), calls=%async_computation.14 | async-start | bytes 3244032 | tf_op jit(solution)/shard_map/all_gather | solution.py:106
  425.0 16.6 %copy-start.113 = (f32[16,4,6]{0,1,2:T(4,128)S(1)}, f32[16,4,6]{0,1,2:T(4,128)}, u32[]{:S(2)}) copy-start(f32[16,4,6]{0,1,2:T(4,128)} %param.30) | copy-start | bytes 4612
  425.0 16.7 %copy-start.137 = (s32[4]{0:T(128)S(1)}, s32[4]{0:T(128)}, u32[]{:S(2)}) copy-start(s32[4]{0:T(128)} %param.28) | copy-start | bytes 52
  425.0 16.9 %copy-start.76 = (bf16[16,4,1536]{2,1,0:T(4,128)(2,1)S(1)}, bf16[16,4,1536]{2,1,0:T(4,128)(2,1)}, u32[]{:S(2)}) copy-start(bf16[16,4,1536]{2,1,0:T(4,128)(2,1)} %param.27) | copy-start | bytes 589828
  425.0 62.5 %all-to-all-start.1 = ((bf16[16,1,48,1536]{3,2,1,0:T(8,128)(2,1)}), bf16[16,1,48,1536]{3,2,1,0:T(8,128)(2,1)}, u32[]{:S(2)}, u32[]{:S(2)}) async-start(bf16[16,1,48,1536]{3,2,1,0:T(8,128)(2,1)} %fusion.10), calls=%async_computation.2 | async-start | bytes 4718592 | tf_op jit(solution)/shard_map/all_to_all | solution.py:279
  448.9 51.0 %copy-start.46 = (bf16[64,1024]{1,0:T(8,128)(2,1)}, bf16[64,1024]{1,0:T(8,128)(2,1)S(1)}, u32[]{:S(2)}) copy-start(bf16[64,1024]{1,0:T(8,128)(2,1)S(1)} %get-tuple-element.275) | copy-start | bytes 393220
  503.3 148.3 %copy-start.24 = (f32[64,1536]{1,0:T(8,128)}, f32[64,1536]{1,0:T(8,128)S(1)}, u32[]{:S(2)}) copy-start(f32[64,1536]{1,0:T(8,128)S(1)} %get-tuple-element.260) | copy-start | bytes 1179652
  514.7 66.6 %copy-start.52 = (f32[16,48,512]{2,1,0:T(8,128)S(1)}, f32[16,48,512]{2,1,0:T(8,128)}, u32[]{:S(2)}) copy-start(f32[16,48,512]{2,1,0:T(8,128)} %copy-done.51) | copy-start | bytes 4718596
  514.7 66.6 %copy-start.54 = (f32[16,48,512]{2,1,0:T(8,128)S(1)}, f32[16,48,512]{2,1,0:T(8,128)}, u32[]{:S(2)}) copy-start(f32[16,48,512]{2,1,0:T(8,128)} %copy-done.53) | copy-start | bytes 4718596
  588.1 49.8 %all-to-all-start.3 = ((bf16[16,1,48,1536]{3,2,1,0:T(8,128)(2,1)}), bf16[16,1,48,1536]{3,2,1,0:T(8,128)(2,1)S(1)}, u32[]{:S(2)}, u32[]{:S(2)}) async-start(bf16[16,1,48,1536]{3,2,1,0:T(8,128)(2,1)} %fusion.11), calls=%async_computation.4 | async-start | bytes 4718592 | tf_op jit(solution)/shard_map/all_to_all | solution.py:332
  592.3 116.6 %all-gather.15.cloned.1.call-start = ((), (), s32[]{:S(2)}) async-start(), calls=%async_computation.15 | async-start | bytes 3342336 | tf_op jit(solution)/shard_map/all_gather | solution.py:392
  651.6 57.4 %copy-start.5 = (f32[256,4,448]{0,2,1:T(8,128)S(1)}, f32[256,4,448]{0,2,1:T(8,128)}, u32[]{:S(2)}) copy-start(f32[256,4,448]{0,2,1:T(8,128)} %copy-done.4) | copy-start | bytes 5505028
  651.6 57.4 %copy-start.43 = (f32[256,4,192]{0,2,1:T(8,128)S(1)}, f32[256,4,192]{0,2,1:T(8,128)}, u32[]{:S(2)}) copy-start(f32[256,4,192]{0,2,1:T(8,128)} %copy-done.42) | copy-start | bytes 2359300
  651.6 57.4 %copy-start.129 = (f32[192]{0:T(256)S(1)}, f32[192]{0:T(256)}, u32[]{:S(2)}) copy-start(f32[192]{0:T(256)} %param.43) | copy-start | bytes 2308
  653.6 60.7 %copy-start.32 = (f32[16,4,1536]{2,1,0:T(4,128)}, f32[16,4,1536]{2,1,0:T(4,128)S(1)}, u32[]{:S(2)}) copy-start(f32[16,4,1536]{2,1,0:T(4,128)S(1)} %reshape.416) | copy-start | bytes 1179652
  655.7 257.0 %reduce-scatter.13.cloned.1.call-start = ((), (), s32[]{:S(2)}) async-start(), calls=%async_computation.16 | async-start | bytes 6684672 | tf_op jit(solution)/shard_map/reduce_scatter | solution.py:458
  741.8 51.1 %copy-start.3 = (f32[259,4,448]{0,2,1:T(8,128)S(1)}, f32[259,4,448]{0,2,1:T(8,128)}, u32[]{:S(2)}) copy-start(f32[259,4,448]{0,2,1:T(8,128)} %copy-done.2) | copy-start | bytes 5569540
  741.8 51.1 %copy-start.21 = (f32[256,4,192]{0,2,1:T(8,128)S(1)}, f32[256,4,192]{0,2,1:T(8,128)}, u32[]{:S(2)}) copy-start(f32[256,4,192]{0,2,1:T(8,128)} %copy-done.20) | copy-start | bytes 2359300
  801.1 14.0 collective-permute-start.1
  827.9 257.5 %reduce-scatter.17.cloned.1.call-start = ((), (), s32[]{:S(2)}) async-start(), calls=%async_computation.18 | async-start | bytes 6488064 | tf_op jit(solution)/shard_map/reduce_scatter | solution.py:502
  832.6 407.5 %reduce-scatter.19.cloned.1.call-start = ((), (), s32[]{:S(2)}) async-start(), calls=%async_computation.19 | async-start | bytes 6488064 | tf_op jit(solution)/shard_map/reduce_scatter | solution.py:503
  837.1 523.1 %reduce-scatter.21.cloned.1.call-start = ((), (), s32[]{:S(2)}) async-start(), calls=%async_computation.20 | async-start | bytes 6488064 | tf_op jit(solution)/shard_map/reduce_scatter | solution.py:504
  841.9 621.0 %reduce-scatter.15.cloned.1.call-start = ((), (), s32[]{:S(2)}) async-start(), calls=%async_computation.17 | async-start | bytes 1622016 | tf_op jit(solution)/shard_map/reduce_scatter | solution.py:498
  850.6 612.3 %all-reduce.29.cloned.1.call-start = ((), (), s32[]{:S(2)}) async-start(), calls=%async_computation.22 | async-start | bytes 25952256 | tf_op jit(solution)/shard_map/psum | solution.py:478
  873.5 83.6 %copy-start.33 = (f32[16,4,1536]{2,1,0:T(4,128)S(1)}, f32[16,4,1536]{2,1,0:T(4,128)}, u32[]{:S(2)}) copy-start(f32[16,4,1536]{2,1,0:T(4,128)} %copy-done.32) | copy-start | bytes 1179652
  (114 other events, 393.9 us)
Sparse Core Ops, SparseCore 0:
  200.6 54.8 reduce-scatter.22
  259.5 94.6 reduce-scatter.10
  655.8 53.0 all-gather.14
  828.0 84.6 reduce-scatter.12
  918.7 166.5 reduce-scatter.16
  1091.4 148.5 reduce-scatter.18
  1246.2 113.9 reduce-scatter.20
  1366.1 96.7 reduce-scatter.14
Sparse Core Ops, SparseCore 1:
  208.4 57.3 all-gather.8
  268.6 85.8 all-gather.10
  368.6 85.9 all-gather.12
  868.5 319.8 all-reduce.28
where the time goes:
time: 1490 us; the launch traced here: 1480 us
  waiting for transfers between devices  816 us (55%)
  blocking collectives  297 us (20%)
  matrix products  135 us (9%)
  other arithmetic  95.2 us (6%)
  local copies, waits for them, and re-layouts  90.2 us (6%)
  starting transfers between devices  31.9 us (2%)
  between operations  17.7 us (1%)
    reduce_scatter x1, waiting for transfers between devices, body(): lax.psum_scatter(shared_up_grad, ('seq', 'mp'), scatter_dimension=0, tile...  155 us
    reduce_scatter x1, waiting for transfers between devices, body(): lax.psum_scatter(shared_gate_grad, ('seq', 'mp'), scatter_dimension=0, ti...  125 us
    reduce_scatter x1, waiting for transfers between devices, body(): lax.psum_scatter(shared_down_grad, ('seq', 'mp'), scatter_dimension=0, ti...  120 us
    reduce_scatter x1, waiting for transfers between devices, body(): lax.psum_scatter(state_proj_grad, ('seq', 'mp'), scatter_dimension=0, til...  103 us
    reduce_scatter x1, waiting for transfers between devices, body(): lax.psum_scatter(mix_part, 'mp', scatter_dimension=0, tiled=True)  97.8 us
    unnamed x2, blocking collectives  83.3 us
    all_to_all x1, blocking collectives, body(): lax.all_to_all(grad_send, 'mp', split_axis=0, concat_axis=0, tiled=True)  66.6 us
    all_to_all x1, waiting for transfers between devices, body(): lax.all_to_all(send_rows, 'mp', split_axis=0, concat_axis=0, tiled=True)  47.1 us
  transfers between devices with their start and end apart: 17, of which 11 were waited for; matrix products, arithmetic and copies ran while one was open for 9% of the time, Pallas kernels for 0%

commit v1 on v0

v1 whole, which is shorter than its diff:
```python
import functools
from types import SimpleNamespace

import jax
import jax.numpy as jnp
from jax import lax
from jax.experimental import pallas as pl
from jax.experimental.pallas import tpu as pltpu
from jax.sharding import PartitionSpec as P

STATE = 128
INNER = 3072


epsilon = 1e-05
highest = lax.Precision.HIGHEST
f32 = jnp.float32
bf16 = jnp.bfloat16


def shifted(block, axis, distance):
    devices = range(lax.axis_size(axis))
    route = [(i - distance, i) for i in devices if i - distance in devices]
    return lax.ppermute(block, axis, route)


def entering_2(value, axis, join, neutral, backward):
    count, mine = (lax.axis_size(axis), lax.axis_index(axis))
    pieces = jax.tree.map(lambda part: lax.all_gather(part, axis), value)
    if backward:
        pieces = jax.tree.map(lambda part: part[::-1], pieces)
        mine = count - 1 - mine
    running = jax.tree.map(
        lambda part, zero: jnp.full_like(part, 0) + jnp.asarray(zero, part.dtype), value, neutral
    )

    def hop(position, running):
        longer = join(running, jax.tree.map(lambda part: part[position], pieces))
        return jax.tree.map(lambda new, old: jnp.where(position < mine, new, old), longer, running)

    return lax.fori_loop(0, count - 1, hop, running)


def rms_scale(values, gain):
    return values * lax.rsqrt(jnp.mean(values * values, axis=-1, keepdims=True) + epsilon) * gain


def silu_slope(values):
    sigmoid_val = jax.nn.sigmoid(values)
    return sigmoid_val * (1.0 + values * (1.0 - sigmoid_val))


def chain_combine(earlier, latter):
    return (earlier[0] * latter[0], latter[0][..., None, None] * earlier[1] + latter[1])


NN = ((1,), (0,))
NT = ((1,), (1,))
TN = ((0,), (0,))
PAD = 8


def mul(a, b, dims, precision=highest):
    return lax.dot_general(a, b, (dims, ((), ())), precision=precision, preferred_element_type=f32)


def iota(shape, axis):
    return lax.broadcasted_iota(jnp.int32, shape, axis)


class Mixer:
    def __init__(self, proj, conv, head, lane, heads, inner):
        self.heads, self.inner, self.dim = heads, inner, inner // heads
        self.iw = lane.shape[1]
        self.ew = self.iw + 2 * STATE
        length = proj.shape[0] - PAD
        self.length, self.window = length, 4
        pre = conv[4:5, :]
        for k in range(self.window):
            pre = pre + conv[k : k + 1, :] * self.tap(proj, k)
        self.pre = pre
        self.sig = jax.nn.sigmoid(pre)
        act = pre * self.sig
        self.v = act[:, : self.iw]
        self.b = act[:, self.iw : self.iw + STATE]
        self.c = act[:, self.iw + STATE :]
        self.raw = proj[PAD:, self.ew + self.iw :] + head[0:1, :]
        self.dt = jnp.maximum(self.raw, 0.0) + jnp.log1p(jnp.exp(-jnp.abs(self.raw)))
        self.rate = -jnp.exp(head[1:2, :])
        self.ld = self.rate * self.dt
        self.mask = iota((length, length), 0) >= iota((length, length), 1)
        self.tri = self.mask.astype(f32)
        self.cum = mul(self.tri, self.ld, NN)
        self.last = self.cum[length - 1 :, :]
        self.gate = proj[PAD:, self.ew : self.ew + self.iw]

    def tap(self, proj, k):
        start = PAD + 1 - self.window + k
        return proj[start : start + self.length, : self.ew]

    def wide(self, x):
        lanes = iota((x.shape[0], self.iw), 1)
        out = jnp.broadcast_to(x[:, self.heads - 1 : self.heads], lanes.shape)
        for h in reversed(range(self.heads - 1)):
            out = jnp.where(lanes < (h + 1) * self.dim, x[:, h : h + 1], out)
        return out

    def narrow(self, x):
        pick = (iota((self.iw, 128), 0) // self.dim == iota((self.iw, 128), 1)).astype(f32)
        return mul(x, pick, NN)

    def of_head(self, x, h):
        return jnp.where(iota(x.shape, 1) // self.dim == h, x, 0.0)

    def decay(self, h, turned):
        gap = self.cum[:, h : h + 1] - turned[h : h + 1, :]
        return jnp.exp(jnp.where(self.mask, gap, -1e30))


def state_kernel(heads, inner, table, proj, conv, head, lane, state_out, total_out):
    m = Mixer(proj, conv, head, lane, heads, inner)
    tail = m.wide(jnp.exp(m.last - m.cum) * m.dt)
    state_out[...] = mul(m.v * tail, m.b, TN)
    total_out[...] = jnp.broadcast_to(jnp.exp(m.last), total_out.shape)


def forward_kernel(heads, inner, table, proj, conv, head, lane, enter, scaled_out, y_out):
    m = Mixer(proj, conv, head, lane, heads, inner)
    scores = mul(m.c, m.b, NT)
    turned = jnp.transpose(m.cum)
    xs = m.v * m.wide(m.dt)
    y = jnp.exp(m.wide(m.cum)) * mul(m.c, enter[...], NT) + lane[0:1, :] * m.v
    for h in range(heads):
        y = y + mul(scores * m.decay(h, turned), m.of_head(xs, h), NN)
    y_out[...] = y
    gated = y * m.gate * jax.nn.sigmoid(m.gate)
    square = jnp.sum(gated * gated, axis=1, keepdims=True)
    high = square.astype(bf16).astype(f32)
    lanes = iota(gated.shape, 1)
    scaled = jnp.where(lanes == inner, high, jnp.where(lanes == inner + 1, square - high, gated * lane[1:2, :]))
    scaled = scaled.astype(bf16)
    count = scaled_out.shape[0]
    size = m.length // count
    for j in range(count):
        scaled_out[table[j]] = scaled[j * size : (j + 1) * size]


def gate_kernel(heads, inner, table, proj, conv, head, lane, y_in, sg_in, enter_grad, dy_out, dgate_out, gain_out, sg):
    m = Mixer(proj, conv, head, lane, heads, inner)
    count = sg_in.shape[0]
    size = m.length // count
    for j in range(count):
        sg[j * size : (j + 1) * size, :] = sg_in[table[j]]
    sum_grad = sg[:, inner : inner + 1] + sg[:, inner + 1 : inner + 2]
    sig = jax.nn.sigmoid(m.gate)
    silu = m.gate * sig
    y = y_in[...]
    gated = y * silu
    grad = sg[...] * lane[1:2, :] + 2.0 * gated * sum_grad
    dy = grad * silu
    dy_out[...] = dy
    dgate_out[...] = (grad * y * sig * (1.0 + m.gate * (1.0 - sig))).astype(bf16)
    gain_out[...] = jnp.broadcast_to(jnp.sum(sg[...] * gated, axis=0, keepdims=True), gain_out.shape)
    enter_grad[...] = mul(jnp.exp(m.wide(m.cum)) * dy, m.c, TN)


def backward_kernel(
    heads, inner, table, proj, conv, head, lane, dy_in, dgate_in, enter_in, exit_in,
    turned_out, plain_out, edge_out, tail_out, sums_out, dpad,
):
    m = Mixer(proj, conv, head, lane, heads, inner)
    length = m.length
    dy, enter, leave = dy_in[...], enter_in[...], exit_in[...]
    scores = mul(m.c, m.b, NT)
    turned = jnp.transpose(m.cum)
    dtw = m.wide(m.dt)
    xs = m.v * dtw
    fade = jnp.exp(m.last - m.cum)
    tail = fade * m.dt
    tailw = m.wide(tail)
    grow = jnp.exp(m.wide(m.cum)) * dy
    dscores = jnp.zeros((length, length), f32)
    dxs = jnp.zeros_like(dy)
    dcum = jnp.zeros((length, 128), f32)
    cols = jnp.zeros((128, length), f32)
    for h in range(heads):
        decay = m.decay(h, turned)
        dyh = m.of_head(dy, h)
        g = mul(dyh, xs, NT)
        weighted = scores * decay
        dscores = dscores + decay * g
        p = weighted * g
        dcum = jnp.where(iota(dcum.shape, 1) == h, jnp.sum(p, axis=1, keepdims=True), dcum)
        cols = jnp.where(iota(cols.shape, 0) == h, jnp.sum(p, axis=0, keepdims=True), cols)
        dxs = dxs + mul(weighted, dyh, TN)
    dcum = dcum - jnp.transpose(cols)
    dc = mul(dscores, m.b, NN) + mul(grow, enter, NN)
    db = mul(dscores, m.c, TN) + mul(tailw * m.v, leave, NN)
    u = mul(m.b, leave, NT)
    dtail = m.narrow(m.v * u)
    dcum = dcum + m.narrow(grow * mul(m.c, enter, NT)) - dtail * tail
    pick = (iota((m.iw, 128), 0) // m.dim == iota((m.iw, 128), 1)).astype(f32)
    total = jnp.sum(mul(enter * leave, pick, TN), axis=0, keepdims=True)
    dlast = jnp.sum(dtail * tail, axis=0, keepdims=True) + total * jnp.exp(m.last)
    dcum = dcum + jnp.where(iota(dcum.shape, 0) == length - 1, dlast, 0.0)
    dld = mul(m.tri, dcum, TN)
    ddt = dtail * fade + m.narrow(dxs * m.v) + m.rate * dld
    dstep = ddt * jax.nn.sigmoid(m.raw)
    dstep = jnp.where(iota(dstep.shape, 1) < heads, dstep, 0.0)
    dv = dxs * dtw + lane[0:1, :] * dy + tailw * u
    dpre = jnp.concatenate([dv, db, dc], axis=1) * (m.sig * (1.0 + m.pre * (1.0 - m.sig)))
    dpad[0:PAD, :] = jnp.zeros((PAD, m.ew), f32)
    dpad[PAD : PAD + length, :] = dpre
    dpad[PAD + length :, :] = jnp.zeros((PAD, m.ew), f32)
    dext = jnp.zeros((length + PAD, m.ew), f32)
    sums_out[...] = jnp.zeros(sums_out.shape, f32)
    for k in range(m.window):
        start = m.window - 1 - k
        dext = dext + conv[k : k + 1, :] * dpad[start : start + length + PAD, :]
        sums_out[k : k + 1, :] = jnp.sum(dpre * m.tap(proj, k), axis=0, keepdims=True)
    sums_out[4:5, :] = jnp.sum(dpre, axis=0, keepdims=True)
    sums_out[5:6, : m.iw] = jnp.sum(dy * m.v, axis=0, keepdims=True)
    sums_out[6:7, :128] = jnp.sum(dstep, axis=0, keepdims=True)
    sums_out[7:8, :128] = jnp.sum(m.ld * dld, axis=0, keepdims=True)
    edge_out[...] = dext[:PAD]
    tail_out[...] = dext[length:]
    low = jnp.concatenate([dext[PAD:].astype(bf16), dgate_in[...], dstep.astype(bf16)], axis=1)
    plain_out[0:PAD, :] = jnp.zeros((PAD, low.shape[1]), bf16)
    plain_out[PAD:, :] = low
    count = turned_out.shape[0]
    size = length // count
    for j in range(count):
        turned_out[table[j]] = low[j * size : (j + 1) * size]


def run_mixer(kernel, heads, inner, table, args, outs, scratch=()):
    count = args[0].shape[0]

    def spec(shape):
        if len(shape) == 2:
            return pl.BlockSpec(shape, lambda b, t: (0, 0))
        if len(shape) == 3:
            return pl.BlockSpec((None,) + shape[1:], lambda b, t: (b, 0, 0))
        return pl.BlockSpec((shape[0], None) + shape[2:], lambda b, t: (0, b, 0, 0))

    return pl.pallas_call(
        functools.partial(kernel, heads, inner),
        grid_spec=pltpu.PrefetchScalarGridSpec(
            num_scalar_prefetch=1,
            grid=(count,),
            in_specs=[spec(a.shape) for a in args],
            out_specs=[spec(o.shape) for o in outs],
            scratch_shapes=list(scratch),
        ),
        out_shape=list(outs),
        name=kernel.__name__,
    )(table, *args)


def swap(block, axis, bit):
    count = lax.axis_size(axis)
    return lax.ppermute(block, axis, [(i, i ^ bit) for i in range(count)])


def bits_of(axis):
    count = lax.axis_size(axis)
    bits = []
    while count > 1:
        count //= 2
        bits.append(count)
    return bits


def positions(order):
    places = [0]
    for bit in order:
        places = places + [place | bit for place in places]
    return places


def spread(block, axis, order):
    held = block[None]
    for bit in order:
        held = jnp.concatenate([held, swap(held, axis, bit)], axis=0)
    return held


def collect(blocks, axis, order, sent=bf16, split=None):
    for bit in reversed(order):
        half = blocks.shape[0] // 2
        going = blocks[half:]
        if split is not None:
            value = going[..., split : split + 1] + going[..., split + 1 : split + 2]
            high = lax.reduce_precision(value, 8, 7)
            column = iota(going.shape, going.ndim - 1)
            going = jnp.where(column == split, high, jnp.where(column == split + 1, value - high, going))
        arrived = swap(going.astype(sent), axis, bit)
        blocks = blocks[:half] + arrived.astype(f32)
    return blocks[0]


def trade(blocks, axis, order):
    count = blocks.shape[0]
    rest = blocks.shape[1:]
    view = blocks.reshape((2,) * len(order) + rest)
    for at, bit in enumerate(order):
        axis_at = len(order) - 1 - at
        kept = lax.index_in_dim(view, 0, axis_at)
        sent = lax.index_in_dim(view, 1, axis_at)
        view = jnp.concatenate([kept, swap(sent, axis, bit)], axis=axis_at)
    return view.reshape((count,) + rest)


def reorder(blocks, axis, order):
    return jnp.take(blocks, lax.axis_index(axis) ^ jnp.array(positions(order), jnp.int32), axis=0)


def absolute(blocks, axis, order):
    places = positions(order)
    inverse = [0] * len(places)
    for at, place in enumerate(places):
        inverse[place] = at
    pick = jnp.array(inverse, jnp.int32)[lax.axis_index(axis) ^ jnp.arange(len(places))]
    return jnp.take(blocks, pick, axis=0)


def spread_all(block):
    seq_bits, mp_bits = bits_of("seq"), bits_of("mp")
    held = absolute(spread(block, "seq", seq_bits), "seq", seq_bits)
    held = absolute(spread(held, "mp", mp_bits), "mp", mp_bits)
    held = jnp.moveaxis(held, 1, 0)
    return held.reshape((-1,) + block.shape)


def collect_all(blocks):
    seq_bits, mp_bits = bits_of("seq"), bits_of("mp")
    rest = blocks.shape[1:]
    view = blocks.reshape((lax.axis_size("seq"), lax.axis_size("mp")) + rest)
    mine = collect(reorder(view, "seq", seq_bits), "seq", seq_bits, f32)
    return collect(reorder(mine, "mp", mp_bits), "mp", mp_bits, f32)


def exchange(value):
    for bit in bits_of("seq"):
        low = value.astype(bf16)
        value = low.astype(f32) + swap(low, "seq", bit).astype(f32)
    return value


def exchange_wide(value):
    for bit in bits_of("seq"):
        value = value + swap(value, "seq", bit)
    return value


def body(
    tokens,
    target,
    lengths,
    routes,
    route_weight,
    in_gain,
    gate_proj,
    value_proj,
    state_proj,
    step_proj,
    conv_value,
    conv_value_bias,
    conv_state,
    conv_state_bias,
    step_bias,
    decay_log,
    skip_gain,
    mixer_gain,
    out_proj,
    ffn_gain,
    shared_gate,
    shared_up,
    shared_down,
    expert_gate,
    routed_up_weights,
    expert_down,
):
    seq_devices, mp_devices = lax.axis_size("seq"), lax.axis_size("mp")
    devices = seq_devices * mp_devices
    me = lax.axis_index("mp")
    slots, sequences, width = tokens.shape
    own = slots // mp_devices
    inner = gate_proj.shape[1]
    heads = step_proj.shape[1]
    window = conv_value.shape[0]
    units = expert_gate.shape[2]
    iw = -(-inner // 128) * 128
    ew = iw + 2 * STATE
    chunks = 2
    per = sequences // chunks
    rows = own * per
    bits, seq_bits = bits_of("mp"), bits_of("seq")
    orders = [bits, bits[2:3] + bits[0:2] + bits[3:]] if len(bits) == 4 else [bits, bits]
    tables = []
    for order in orders:
        places = positions(order)
        inverse = [places.index(at) for at in range(mp_devices)]
        tables.append(jnp.array(inverse, jnp.int32)[me ^ jnp.arange(mp_devices)].astype(jnp.int32))

    edge_tokens = shifted(tokens[slots - window + 1 :], "seq", 1)
    x_seq = jnp.concatenate([jnp.zeros((PAD + 1 - window,) + tokens.shape[1:], bf16), edge_tokens, tokens], axis=0)
    x_seq = jnp.transpose(x_seq, (1, 0, 2))
    d_rows = in_gain.shape[0]
    c_rows = conv_state_bias.shape[0]
    small = jnp.concatenate([in_gain, ffn_gain, conv_state.reshape(-1), conv_state_bias])
    small = jnp.pad(small, (0, -small.shape[0] % 128))
    small_all = spread_all(small)
    in_gain_all = small_all[:, :d_rows].reshape(width).astype(f32)
    ffn_gain_all = small_all[:, d_rows : 2 * d_rows].reshape(width).astype(f32)
    at = 2 * d_rows + window * c_rows
    conv_state_all = small_all[:, 2 * d_rows : at].reshape(2 * STATE, window).astype(f32)
    conv_bias_all = small_all[:, at : at + c_rows].reshape(2 * STATE).astype(f32)
    state_all = spread_all(state_proj).reshape(width, 2 * STATE)
    w_all = jnp.concatenate(
        [
            jnp.pad(value_proj, ((0, 0), (0, iw - inner))),
            state_all,
            jnp.pad(gate_proj, ((0, 0), (0, iw - inner))),
            jnp.pad(step_proj, ((0, 0), (0, 128 - heads))),
        ],
        axis=1,
    )
    conv_all = jnp.concatenate(
        [
            jnp.pad(jnp.concatenate([conv_value, conv_value_bias[None]]), ((0, 7 - window), (0, iw - inner))),
            jnp.pad(jnp.concatenate([conv_state_all.T, conv_bias_all[None]]), ((0, 7 - window), (0, 0))),
        ],
        axis=1,
    )
    head_all = jnp.pad(jnp.stack([step_bias, decay_log]), ((0, 6), (0, 128 - heads)))
    lane_all = jnp.pad(jnp.stack([jnp.repeat(skip_gain, inner // heads), mixer_gain]), ((0, 6), (0, iw - inner)))
    out_all = jnp.pad(out_proj, ((0, iw - inner), (0, 128)))
    r, c = iota(out_all.shape, 0), iota(out_all.shape, 1)
    out_all = jnp.where((c >= width) & (c < width + 2) & (r - inner == c - width), 1.0, out_all).astype(bf16)

    ipd = shared_down.shape[0]
    extra = ipd * seq_devices
    pair = jnp.stack([shared_gate, shared_up], 0).reshape(2, d_rows, seq_devices, mp_devices, ipd)
    pair = jnp.transpose(pair, (3, 1, 0, 2, 4)).reshape(mp_devices, d_rows, 2 * extra)
    pair = absolute(trade(reorder(pair, "mp", bits), "mp", bits), "mp", bits)
    pair = absolute(spread(pair, "seq", seq_bits), "seq", seq_bits).reshape(width, 2 * extra)
    down_slice = absolute(spread(shared_down, "seq", seq_bits), "seq", seq_bits).reshape(extra, width)
    w_gate = jnp.concatenate([expert_gate[0], pair[:, :extra]], axis=1)
    w_up = jnp.concatenate([routed_up_weights[0], pair[:, extra:]], axis=1)
    w_down = jnp.concatenate([expert_down[0], down_slice], axis=0)

    named = routes[..., None] == jnp.arange(mp_devices, dtype=jnp.int32)
    coefficient = jnp.sum(jnp.where(named, route_weight[..., None], 0.0), axis=2)
    coefficient = jnp.transpose(coefficient, (1, 0, 2)).reshape(chunks, rows, mp_devices)
    row_coef = []
    for g in range(chunks):
        every = spread(coefficient[g], "mp", orders[g]).reshape(mp_devices * rows, mp_devices)
        mine = jnp.sum(jnp.where(jnp.arange(mp_devices) == me, every, 0.0), axis=1)
        row_coef.append(jnp.where(jnp.arange(units + extra)[None, :] < units, mine[:, None], 1.0))

    targets = jnp.transpose(target, (1, 0, 2)).astype(f32).reshape(chunks, rows, width)
    position = lax.axis_index("seq") * slots + me * own + jnp.arange(own, dtype=jnp.int32)
    valid = (position[None, :] < lengths[:, None]).astype(f32).reshape(chunks, rows, 1)

    def struct(shape, kind=f32):
        return jax.ShapeDtypeStruct(shape, kind)

    def passing(total, state, backward):
        if seq_devices == 2:
            return shifted(state, "seq", -1 if backward else 1)
        split = state[:, :inner].reshape(per, heads, inner // heads, STATE)
        decay = total[:, 0, :heads]
        got = entering_2((decay, split), "seq", chain_combine, (jnp.ones_like(decay), jnp.zeros_like(split)), backward)
        return jnp.pad(got[1].reshape(per, inner, STATE), ((0, 0), (0, iw - inner), (0, 0)))

    kept = [SimpleNamespace() for _ in range(chunks)]
    for g, k in enumerate(kept):
        x = x_seq[g * per : (g + 1) * per]
        k.normed = rms_scale(x.astype(f32), in_gain_all).astype(bf16).reshape(per * (slots + PAD), width)
        proj = mul(k.normed, w_all, NN, None).reshape(per, slots + PAD, w_all.shape[1])
        k.shared = (proj, conv_all, head_all, lane_all)
        state, k.total = run_mixer(
            state_kernel, heads, inner, tables[g], k.shared, [struct((per, iw, STATE)), struct((per, 8, 128))]
        )
        k.entering = passing(k.total, state, False)
    for g, k in enumerate(kept):
        k.scaled, k.y = run_mixer(
            forward_kernel,
            heads,
            inner,
            tables[g],
            k.shared + (k.entering,),
            [struct((mp_devices, per, own, iw), bf16), struct((per, slots, iw))],
        )
        k.scaled = k.scaled.reshape(mp_devices * rows, iw)
        part = mul(k.scaled, out_all, NN, None).reshape(mp_devices, rows, -1)
        mixed = collect(part, "mp", orders[g], split=width)
        k.pre_mix = mixed[:, :width]
        k.inv_norm = lax.rsqrt((mixed[:, width : width + 1] + mixed[:, width + 1 : width + 2]) / INNER + epsilon)
        k.own = lax.dynamic_slice(x_seq, (g * per, PAD + me * own, 0), (per, own, width)).astype(f32).reshape(rows, width)
        k.hidden = k.own + k.pre_mix * k.inv_norm
        ffn_own = rms_scale(k.hidden, ffn_gain_all).astype(bf16)
        k.ffn = spread(ffn_own, "mp", orders[g]).reshape(mp_devices * rows, width)
    for g, k in enumerate(kept):
        k.g = mul(k.ffn, w_gate, NN, None)
        k.u = mul(k.ffn, w_up, NN, None)
        k.act = (row_coef[g] * jax.nn.silu(k.g) * k.u).astype(bf16)
        part = mul(k.act, w_down, NN, None).reshape(mp_devices, rows, width)
        output = k.hidden + collect(part, "mp", orders[g])
        k.out = output.astype(bf16)
        k.grad_out = (output - targets[g]) * valid[g]
        k.grad_low = spread(k.grad_out.astype(bf16), "mp", orders[g]).reshape(mp_devices * rows, width)
    for g, k in enumerate(kept):
        back = mul(k.grad_low, w_down, NT, None) * row_coef[g]
        k.dg = (back * k.u * silu_slope(k.g)).astype(bf16)
        k.du = (back * jax.nn.silu(k.g)).astype(bf16)
        part = mul(k.dg, w_gate, NT, None) + mul(k.du, w_up, NT, None)
        ffn_grad = collect(part.reshape(mp_devices, rows, width), "mp", orders[g])
        _, norm_back = jax.vjp(rms_scale, k.hidden, ffn_gain_all)
        hidden_part, k.ffn_gain_grad = norm_back(ffn_grad)
        k.hidden_grad = k.grad_out + hidden_part
        sum_share = (
            jnp.sum(k.hidden_grad * k.pre_mix, axis=-1, keepdims=True)
            * (-0.5 / INNER) * k.inv_norm * k.inv_norm * k.inv_norm
        )
        high = lax.reduce_precision(sum_share, 8, 7)
        lane = jnp.arange(128)
        more = jnp.where(lane == 0, high, jnp.where(lane == 1, sum_share - high, 0.0))
        packed = jnp.concatenate([k.hidden_grad * k.inv_norm, more], axis=-1).astype(bf16)
        k.mix = spread(packed, "mp", orders[g]).reshape(mp_devices * rows, width + 128)
    for g, k in enumerate(kept):
        scaled_grad = mul(k.mix, out_all, NT, None).reshape(mp_devices, per, own, iw)
        k.enter_grad, k.dy, k.dgate, k.gain_sum = run_mixer(
            gate_kernel,
            heads,
            inner,
            tables[g],
            k.shared + (k.y, scaled_grad),
            [struct((per, iw, STATE)), struct((per, slots, iw)), struct((per, slots, iw), bf16), struct((per, 8, iw))],
            [pltpu.VMEM((slots, iw), f32)],
        )
        k.leaving = passing(k.total, k.enter_grad, True)

    def both(a, b):
        return mul(jnp.concatenate(a, 0), jnp.concatenate(b, 0), TN, None)

    d_down = both([k.act for k in kept], [k.grad_low for k in kept])
    d_gate = both([k.ffn for k in kept], [k.dg for k in kept])
    d_up = both([k.ffn for k in kept], [k.du for k in kept])
    expert_gate_grad = exchange(d_gate[:, :units])[None]
    expert_up_grad = exchange(d_up[:, :units])[None]
    expert_down_grad = exchange(d_down[:units])[None]
    d_pair = jnp.concatenate([d_gate[:, units:], d_up[:, units:]], axis=1)
    d_pair = d_pair.reshape(seq_devices, mp_devices, d_rows, 2 * extra)
    d_pair = collect(reorder(d_pair, "seq", seq_bits), "seq", seq_bits)
    d_pair = reorder(d_pair.astype(bf16), "mp", bits)
    d_pair = absolute(trade(d_pair, "mp", bits), "mp", bits).astype(f32)
    d_pair = d_pair.reshape(mp_devices, d_rows, 2, seq_devices, ipd)
    d_pair = jnp.transpose(d_pair, (2, 1, 3, 0, 4)).reshape(2, d_rows, devices * ipd)
    d_down_own = d_down[units:].reshape(seq_devices, ipd, width)
    shared_down_grad = collect(reorder(d_down_own, "seq", seq_bits), "seq", seq_bits)

    for g, k in enumerate(kept):
        columns = w_all.shape[1]
        turned, plain, edge, tail, k.sums = run_mixer(
            backward_kernel,
            heads,
            inner,
            tables[g],
            k.shared + (k.dy, k.dgate, k.entering, k.leaving),
            [
                struct((mp_devices, per, own, columns), bf16),
                struct((per, slots + PAD, columns), bf16),
                struct((per, PAD, ew)),
                struct((per, PAD, ew)),
                struct((per, 8, ew)),
            ],
            [pltpu.VMEM((slots + 2 * PAD, ew), f32)],
        )
        end = (tail + shifted(edge, "seq", -1)).astype(bf16)
        k.plain = lax.dynamic_update_slice(plain, end, (0, slots, 0)).reshape(per * (slots + PAD), columns)
        turned = lax.dynamic_update_slice(turned, end[None], (tables[g][mp_devices - 1], 0, own - PAD, 0))
        part = mul(turned.reshape(mp_devices * rows, columns), w_all, NT, None)
        normed_grad = collect(part.reshape(mp_devices, rows, width), "mp", orders[g])
        _, first_norm_back = jax.vjp(lambda v: rms_scale(v, in_gain_all), k.own)
        k.tokens_grad = first_norm_back(normed_grad)[0] + k.hidden_grad

    def whole(pieces):
        return jnp.transpose(jnp.concatenate(pieces, 0).reshape(sequences, own, width), (1, 0, 2))

    block_out = whole([k.out for k in kept])
    tokens_grad = whole([k.tokens_grad for k in kept])
    d_out = both([k.scaled for k in kept], [k.mix for k in kept])[:inner, :width]
    d_all = both([k.normed for k in kept], [k.plain for k in kept])
    in_gain_part = jnp.sum(d_all * w_all.astype(f32), axis=1) / in_gain_all
    sums = sum(jnp.sum(k.sums, axis=0) for k in kept)
    gain_sum = sum(jnp.sum(k.gain_sum, axis=0) for k in kept)
    ffn_gain_part = sum(k.ffn_gain_grad for k in kept)
    out_proj_grad = exchange(d_out)
    gate_at = ew + iw
    head_grads = exchange(
        jnp.concatenate([d_all[:, ew : ew + inner], d_all[:, :inner], d_all[:, gate_at : gate_at + heads]], axis=1)
    )
    packed = jnp.concatenate(
        [
            d_all[:, iw:ew].reshape(devices, d_rows * 2 * STATE),
            in_gain_part.reshape(devices, d_rows),
            ffn_gain_part.reshape(devices, d_rows),
            sums[:window, iw:].T.reshape(devices, c_rows * window),
            sums[window, iw:].reshape(devices, c_rows),
        ],
        axis=1,
    )
    packed = jnp.pad(packed, ((0, 0), (0, -packed.shape[1] % 1024))).reshape(devices, -1, 128)
    mine = collect_all(packed).reshape(-1)
    parts, at = [], 0
    for size in (d_rows * 2 * STATE, d_rows, d_rows, c_rows * window, c_rows):
        parts.append(mine[at : at + size])
        at += size
    skips = jnp.sum(sums[5, :inner].reshape(heads, -1), axis=1)
    tiny = jnp.concatenate(
        [sums[: window + 1, :inner].reshape(-1), gain_sum[0, :inner], sums[6, :heads], sums[7, :heads], skips]
    )
    tiny = exchange_wide(tiny)
    at = window * inner
    ends = at + 2 * inner
    return (
        block_out,
        tokens_grad,
        parts[1],
        head_grads[:, :inner],
        head_grads[:, inner : 2 * inner],
        parts[0].reshape(d_rows, 2 * STATE),
        head_grads[:, 2 * inner :],
        tiny[:at].reshape(window, inner),
        tiny[at : at + inner],
        parts[3].reshape(c_rows, window),
        parts[4],
        tiny[ends : ends + heads],
        tiny[ends + heads : ends + 2 * heads],
        tiny[ends + 2 * heads :],
        tiny[at + inner : ends],
        out_proj_grad,
        parts[2],
        d_pair[0],
        d_pair[1],
        shared_down_grad,
        expert_gate_grad,
        expert_up_grad,
        expert_down_grad,
    )


def solution(mesh):
    placed = (
        P("seq", None, None),
        P(("seq", "mp"), None, None),
        P(),
        P(("seq", "mp"), None, None),
        P(("seq", "mp"), None, None),
        P(("seq", "mp")),
        P(None, "mp"),
        P(None, "mp"),
        P(("seq", "mp"), None),
        P(None, "mp"),
        P(None, "mp"),
        P("mp"),
        P(("seq", "mp"), None),
        P(("seq", "mp")),
        P("mp"),
        P("mp"),
        P("mp"),
        P("mp"),
        P("mp", None),
        P(("seq", "mp")),
        P(("seq", "mp"), None),
        P(("seq", "mp"), None),
        P(("seq", "mp"), None),
        P("mp", None, None),
        P("mp", None, None),
        P("mp", None, None),
    )
    return jax.shard_map(
        body,
        mesh=mesh,
        in_specs=placed,
        out_specs=(
            P(("seq", "mp"), None, None),
            P(("seq", "mp"), None, None),
            P(("seq", "mp")),
            P(None, "mp"),
            P(None, "mp"),
            P(("seq", "mp"), None),
            P(None, "mp"),
            P(None, "mp"),
            P("mp"),
            P(("seq", "mp"), None),
            P(("seq", "mp")),
            P("mp"),
            P("mp"),
            P("mp"),
            P("mp"),
            P("mp", None),
            P(("seq", "mp")),
            P(("seq", "mp"), None),
            P(("seq", "mp"), None),
            P(("seq", "mp"), None),
            P("mp", None, None),
            P("mp", None, None),
            P("mp", None, None),
        ),
        check_vma=False,
    )
```

time: 1490 us -> 709 us (0.48)
  waiting for transfers between devices: 816 us -> 244 us
  blocking collectives: 297 us -> 0 us
  matrix products: 135 us -> 54.9 us
  Pallas kernels: 0 us -> 67.1 us
  starting transfers between devices: 31.9 us -> 92.4 us
  local copies, waits for them, and re-layouts: 90.2 us -> 139 us
    reduce_scatter x6 -> x0, waiting for transfers between devices: 624 us -> none  [the longest x1 155 us: body(): lax.psum_scatter(shared_up_grad, ('seq', 'mp'), scatter_dimension=0, tile...]
    ppermute x0 -> x97, waiting for transfers between devices: none -> 244 us  [swap(): return lax.ppermute(block, axis, [(i, i ^ bit) for i in range(count)])]
    all_gather x6 -> x0, blocking collectives: 135 us -> none  [the longest x1 42.6 us: gather_shared(): lax.all_gather(state_proj, ('seq', 'mp'), axis=0, tiled=True)]
    all_to_all x3 -> x0, waiting for transfers between devices: 128 us -> none  [the longest x1 47.1 us: body(): lax.all_to_all(send_rows, 'mp', split_axis=0, concat_axis=0, tiled=True)]
    unnamed x2 -> x0, blocking collectives: 83.3 us -> none
    ppermute x0 -> x97, starting transfers between devices: none -> 80.3 us  [swap(): return lax.ppermute(block, axis, [(i, i ^ bit) for i in range(count)])]
    dot_general x45 -> x25, matrix products: 135 us -> 54.9 us  [mul(): lax.dot_general(a, b, (dims, ((), ())), precision=precision, preferred_el...]
    pallas_call x0 -> x8, Pallas kernels: none -> 67.1 us  [run_mixer(): pl.pallas_call(functools.partial(kernel, heads, inner), grid_spec=pltpu.P...]
  transfers between devices with their start and end apart: 17 -> 104, of which waited for: 11 -> 55; matrix products, arithmetic and copies ran while one was open for 9% -> 35% of each run, Pallas kernels for 0% -> 10%
where the time goes in v1:
time: 709 us; the launch traced here: 701 us
  waiting for transfers between devices  244 us (34%)
  local copies, waits for them, and re-layouts  139 us (20%)
  other arithmetic  95.4 us (13%)
  starting transfers between devices  92.4 us (13%)
  Pallas kernels  67.1 us (9%)
  matrix products  54.9 us (8%)
  between operations  8.2 us (1%)
    ppermute x97, waiting for transfers between devices, swap(): return lax.ppermute(block, axis, [(i, i ^ bit) for i in range(count)])  244 us
    ppermute x97, starting transfers between devices, swap(): return lax.ppermute(block, axis, [(i, i ^ bit) for i in range(count)])  80.3 us
    pallas_call x8, Pallas kernels, run_mixer(): pl.pallas_call(functools.partial(kernel, heads, inner), grid_spec=pltpu.P...  67.1 us
    dot_general x25, matrix products, mul(): lax.dot_general(a, b, (dims, ((), ())), precision=precision, preferred_el...  54.9 us
    unnamed x376, local copies, waits for them, and re-layouts  54.4 us
  transfers between devices with their start and end apart: 104, of which 55 were waited for; matrix products, arithmetic and copies ran while one was open for 35% of the time, Pallas kernels for 10%

profile of v1, /device:TPU:0, one launch (start us, length us, event | category | flops | bytes accessed | tf_op | source)
XLA Modules:
  0.0 701.0 jit_solution(11198192978408495286)
XLA Ops:
  51.5 3.2 collective-permute-start
  65.3 3.5 collective-permute-done.40
  96.8 3.4 pad_maximum_fusion
  103.1 4.0 collective-permute-done.8
  107.8 5.5 collective-permute-done.9
  123.7 3.1 fusion.25.proj
  126.7 5.5 state_kernel.3
  133.5 4.5 fusion.27.proj
  138.1 5.6 state_kernel.2
  146.1 7.7 %forward_kernel.3 = (bf16[16,2,16,256]{3,2,1,0:T(8,128)(2,1)}, f32[2,256,256]{2,1,0:T(8,128)}) custom-call(s32[16]{0:T(128)} %copy-done.102, f32[2,264,896]{2,1,0:T(8,128)} %fusion.25.proj, f32[8,512]{1,0:T(8,128)} %pad_maximum_fusion.49.conv, f32[8,128]{1,0:T(8,128)} %select_maximum_fusion.2.head, f32[8,256]{1,0:T(8,128)} %select_maximum_fusion.lane, ...), custom_call_target="tpu_custom_call" | custom-call | tf_op jit(solution)/shard_map/forward_kernel/pallas_call | solution.py:246
  155.8 7.8 %forward_kernel.2 = (bf16[16,2,16,256]{3,2,1,0:T(8,128)(2,1)}, f32[2,256,256]{2,1,0:T(8,128)}) custom-call(s32[16]{0:T(128)} %copy-done.103, f32[2,264,896]{2,1,0:T(8,128)} %fusion.27.proj, f32[8,512]{1,0:T(8,128)} %pad_maximum_fusion.49.conv, f32[8,128]{1,0:T(8,128)} %select_maximum_fusion.2.head, f32[8,256]{1,0:T(8,128)} %select_maximum_fusion.lane, ...), custom_call_target="tpu_custom_call" | custom-call | tf_op jit(solution)/shard_map/forward_kernel/pallas_call | solution.py:246
  204.2 7.7 %collective-permute-done.36 = bf16[4,32,1664]{2,1,0:T(8,128)(2,1)S(1)} collective-permute-done((bf16[4,32,1664]{2,1,0:T(8,128)(2,1)}, bf16[4,32,1664]{2,1,0:T(8,128)(2,1)S(1)}, u32[]{:S(2)}, u32[]{:S(2)}) %collective-permute-start.36) | collective-permute-done | bytes 426016 | tf_op jit(solution)/shard_map/ppermute | solution.py:262
  214.7 6.8 collective-permute-done.14
  221.8 4.2 collective-permute-done.37
  228.3 4.1 collective-permute-done.15
  242.9 3.1 collective-permute-done.21
  254.8 3.3 collective-permute-done.45
  276.7 7.5 %collective-permute-done.31 = bf16[4,32,1536]{2,1,0:T(8,128)(2,1)S(1)} collective-permute-done((bf16[4,32,1536]{2,1,0:T(8,128)(2,1)S(1)}, bf16[4,32,1536]{2,1,0:T(8,128)(2,1)S(1)}, u32[]{:S(2)}, u32[]{:S(2)}) %collective-permute-start.31) | collective-permute-done | bytes 393248 | tf_op jit(solution)/shard_map/ppermute | solution.py:262
  288.3 5.8 collective-permute-done.32
  294.8 6.1 collective-permute-done.49
  302.6 3.4 collective-permute-done.50
  311.0 9.3 %collective-permute-done.70 = bf16[2,32,1536]{2,1,0:T(8,128)(2,1)S(1)} collective-permute-done((bf16[2,32,1536]{2,1,0:T(8,128)(2,1)S(1)}, bf16[2,32,1536]{2,1,0:T(8,128)(2,1)S(1)}, u32[]{:S(2)}, u32[]{:S(2)}) %collective-permute-start.70) | collective-permute-done | bytes 196640 | tf_op jit(solution)/shard_map/ppermute | solution.py:262
  322.7 5.9 collective-permute-done.71
  346.8 3.4 fusion.157
  350.2 3.3 collective-permute-done.95
  355.6 4.1 convolution_add_fusion
  373.3 3.2 slice.1294
  376.5 3.3 slice.1293
  396.3 8.6 %collective-permute-done.56 = bf16[4,32,1536]{2,1,0:T(8,128)(2,1)S(1)} collective-permute-done((bf16[4,32,1536]{2,1,0:T(8,128)(2,1)S(1)}, bf16[4,32,1536]{2,1,0:T(8,128)(2,1)S(1)}, u32[]{:S(2)}, u32[]{:S(2)}) %collective-permute-start.56) | collective-permute-done | bytes 393248 | tf_op jit(solution)/shard_map/ppermute | solution.py:262
  408.1 5.3 collective-permute-done.57
  413.7 7.0 collective-permute-done.75
  432.8 4.5 add_bitcast_fusion
  437.3 15.8 %collective-permute-done.102 = bf16[1536,512]{0,1:T(8,128)(2,1)} collective-permute-done((bf16[1536,512]{0,1:T(8,128)(2,1)}, bf16[1536,512]{0,1:T(8,128)(2,1)}, u32[]{:S(2)}, u32[]{:S(2)}) %collective-permute-start.102) | collective-permute-done | bytes 1572896 | tf_op jit(solution)/shard_map/ppermute | solution.py:262
  455.9 27.9 %collective-permute-done.101 = bf16[1536,512]{0,1:T(8,128)(2,1)} collective-permute-done((bf16[1536,512]{0,1:T(8,128)(2,1)}, bf16[1536,512]{0,1:T(8,128)(2,1)}, u32[]{:S(2)}, u32[]{:S(2)}) %collective-permute-start.101) | collective-permute-done | bytes 1572896 | tf_op jit(solution)/shard_map/ppermute | solution.py:262
  483.8 4.9 add_bitcast_fusion.2
  491.0 3.6 copy.231
  507.9 3.8 collective-permute-done.61
  517.8 5.4 gate_kernel.2
  525.5 3.1 fusion.54.sg_in
  528.6 5.4 gate_kernel.3
  545.3 14.8 %backward_kernel.2 = (bf16[16,2,16,896]{3,2,1,0:T(8,128)(2,1)}, bf16[2,264,896]{2,1,0:T(8,128)(2,1)}, f32[2,8,512]{2,1,0:T(8,128)}, f32[2,8,512]{2,1,0:T(8,128)}, f32[2,8,512]{2,1,0:T(8,128)}) custom-call(s32[16]{0:T(128)} %copy-done.103, f32[2,264,896]{2,1,0:T(8,128)} %fusion.27.proj, f32[8,512]{1,0:T(8,128)} %pad_maximum_fusion.49.conv, ...), custom_call_target="tpu_custom_call" | custom-call | tf_op jit(solution)/shard_map/backward_kernel/pallas_call | solution.py:246
  561.5 15.0 %backward_kernel.3 = (bf16[16,2,16,896]{3,2,1,0:T(8,128)(2,1)}, bf16[2,264,896]{2,1,0:T(8,128)(2,1)}, f32[2,8,512]{2,1,0:T(8,128)}, f32[2,8,512]{2,1,0:T(8,128)}, f32[2,8,512]{2,1,0:T(8,128)}) custom-call(s32[16]{0:T(128)} %copy-done.102, f32[2,264,896]{2,1,0:T(8,128)} %fusion.25.proj, f32[8,512]{1,0:T(8,128)} %pad_maximum_fusion.49.conv, ...), custom_call_target="tpu_custom_call" | custom-call | tf_op jit(solution)/shard_map/backward_kernel/pallas_call | solution.py:246
  596.1 3.9 fusion.184
  602.5 6.4 copy.222
  628.7 28.9 %collective-permute-done.87 = f32[1,16,104,128]{3,2,1,0:T(8,128)S(1)} collective-permute-done((f32[1,16,104,128]{3,2,1,0:T(8,128)S(1)}, f32[1,16,104,128]{3,2,1,0:T(8,128)S(1)}, u32[]{:S(2)}, u32[]{:S(2)}) %collective-permute-start.87) | collective-permute-done | bytes 852000 | tf_op jit(solution)/shard_map/ppermute | solution.py:262
  677.9 3.9 collective-permute-done.86
  687.4 3.8 collective-permute-done.90
  692.8 3.8 collective-permute-done.91
  (937 shorter events, 379.0 us)
Async XLA Ops:
  2.4 33.8 %collective-permute-start.1 = (bf16[1,256]{1,0:T(2,128)(2,1)S(1)}, bf16[1,256]{1,0:T(2,128)(2,1)S(1)}, u32[]{:S(2)}, u32[]{:S(2)}) collective-permute-start(bf16[1,256]{1,0:T(2,128)(2,1)S(1)} %broadcast_in_dim.494), channel_id=1, source_target_pairs={{0,16},{16,0},{1,17},{17,1},{2,18},{18,2},{3,19},{19,3},{4,20},{20... | collective-permute-start | bytes 1544 | tf_op jit(solution)/shard_map/ppermute | solution.py:262
  7.1 44.4 %collective-permute-start.16 = (f32[1,32,16]{1,2,0:T(8,128)S(1)}, f32[1,32,16]{1,2,0:T(8,128)}, u32[]{:S(2)}, u32[]{:S(2)}) collective-permute-start(f32[1,32,16]{1,2,0:T(8,128)S(1)} %copy.209), channel_id=1, source_target_pairs={{0,8},{1,9},{2,10},{3,11},{4,12},{5,13},{6,14},{7,15},{8,0},{9,1},... | collective-permute-start | bytes 6152 | tf_op jit(solution)/shard_map/ppermute | solution.py:262
  9.8 45.7 %collective-permute-start.39 = (f32[1,32,16]{1,2,0:T(8,128)S(1)}, f32[1,32,16]{1,2,0:T(8,128)}, u32[]{:S(2)}, u32[]{:S(2)}) collective-permute-start(f32[1,32,16]{1,2,0:T(8,128)S(1)} %copy.217), channel_id=1, source_target_pairs={{0,2},{1,3},{2,0},{3,1},{4,6},{5,7},{6,4},{7,5},{8,10},{9,11},{10,... | collective-permute-start | bytes 6152 | tf_op jit(solution)/shard_map/ppermute | solution.py:262
  11.3 80.1 %collective-permute-start.6 = (bf16[1,48,256]{2,1,0:T(8,128)(2,1)}, bf16[1,48,256]{2,1,0:T(8,128)(2,1)}, u32[]{:S(2)}, u32[]{:S(2)}) collective-permute-start(bf16[1,48,256]{2,1,0:T(8,128)(2,1)} %bitcast.381), channel_id=1, source_target_pairs={{0,16},{16,0},{1,17},{17,1},{2,18},{18,2},{3,19},{19,3},{4,20},{20... | collective-permute-start | bytes 73736 | tf_op jit(solution)/shard_map/ppermute | solution.py:262
  11.8 179.1 %collective-permute-start.29 = (bf16[1,32,1536]{2,1,0:T(8,128)(2,1)}, bf16[1,32,1536]{2,1,0:T(8,128)(2,1)}, u32[]{:S(2)}, u32[]{:S(2)}) collective-permute-start(bf16[1,32,1536]{2,1,0:T(8,128)(2,1)} %bitcast.377), channel_id=1, source_target_pairs={{0,16},{16,0},{1,17},{17,1},{2,18},{18,2},{3,19},{19,3},{4,20},{20... | collective-permute-start | bytes 294920 | tf_op jit(solution)/shard_map/ppermute | solution.py:262
  47.0 126.9 %collective-permute-start.24 = (bf16[2,2,2,1,48,128]{5,4,3,2,1,0:T(8,128)(2,1)}, bf16[2,2,2,1,48,128]{5,4,3,2,1,0:T(8,128)(2,1)}, u32[]{:S(2)}, u32[]{:S(2)}) collective-permute-start(bf16[2,2,2,1,48,128]{5,4,3,2,1,0:T(8,128)(2,1)} %copy.235), channel_id=1, source_target_pairs={{0,8},{1,9},{2,10},{3,11},{4,12},{5,13},{6,14},{7,15},{8,0},{9,1},... | collective-permute-start | bytes 294920 | tf_op jit(solution)/shard_map/ppermute | solution.py:262
  51.5 44.9 %collective-permute-start = (bf16[3,4,1536]{2,0,1:T(4,128)(2,1)}, bf16[3,4,1536]{2,0,1:T(4,128)(2,1)}, u32[]{:S(2)}, u32[]{:S(2)}) collective-permute-start(bf16[3,4,1536]{2,0,1:T(4,128)(2,1)} %slice.812), channel_id=1, source_target_pairs={{0,16},{1,17},{2,18},{3,19},{4,20},{5,21},{6,22},{7,23},{8,24},{9,... | collective-permute-start | bytes 110600 | tf_op jit(solution)/shard_map/ppermute | solution.py:24
  81.6 90.8 %collective-permute-start.42 = (f32[8,32,16]{1,2,0:T(8,128)}, f32[8,32,16]{1,2,0:T(8,128)}, u32[]{:S(2)}, u32[]{:S(2)}) collective-permute-start(f32[8,32,16]{1,2,0:T(8,128)} %pad_maximum_fusion.45), channel_id=1, source_target_pairs={{0,1},{1,0},{2,3},{3,2},{4,5},{5,4},{6,7},{7,6},{8,9},{9,8},{10,11... | collective-permute-start | bytes 49160 | tf_op jit(solution)/shard_map/ppermute | solution.py:262
  91.4 84.0 %collective-permute-start.19 = (f32[8,32,16]{1,2,0:T(8,128)}, f32[8,32,16]{1,2,0:T(8,128)}, u32[]{:S(2)}, u32[]{:S(2)}) collective-permute-start(f32[8,32,16]{1,2,0:T(8,128)} %pad_maximum_fusion.44), channel_id=1, source_target_pairs={{0,1},{1,0},{2,3},{3,2},{4,5},{5,4},{6,7},{7,6},{8,9},{9,8},{10,11... | collective-permute-start | bytes 49160 | tf_op jit(solution)/shard_map/ppermute | solution.py:262
  132.2 11.5 %collective-permute-start.34 = (f32[2,256,128]{2,1,0:T(8,128)}, f32[2,256,128]{2,1,0:T(8,128)S(1)}, u32[]{:S(2)}, u32[]{:S(2)}) collective-permute-start(f32[2,256,128]{2,1,0:T(8,128)} %get-tuple-element.50), channel_id=1, source_target_pairs={{0,16},{1,17},{2,18},{3,19},{4,20},{5,21},{6,22},{7,23},{8,24},{9,... | collective-permute-start | bytes 786440 | tf_op jit(solution)/shard_map/ppermute | solution.py:24
  143.7 12.1 %collective-permute-start.11 = (f32[2,256,128]{2,1,0:T(8,128)}, f32[2,256,128]{2,1,0:T(8,128)}, u32[]{:S(2)}, u32[]{:S(2)}) collective-permute-start(f32[2,256,128]{2,1,0:T(8,128)} %get-tuple-element.48), channel_id=1, source_target_pairs={{0,16},{1,17},{2,18},{3,19},{4,20},{5,21},{6,22},{7,23},{8,24},{9,... | collective-permute-start | bytes 786440 | tf_op jit(solution)/shard_map/ppermute | solution.py:24
  170.6 14.3 %collective-permute-start.12 = (bf16[8,32,1664]{2,1,0:T(8,128)(2,1)}, bf16[8,32,1664]{2,1,0:T(8,128)(2,1)S(1)}, u32[]{:S(2)}, u32[]{:S(2)}) collective-permute-start(bf16[8,32,1664]{2,1,0:T(8,128)(2,1)} %get-tuple-element.314), channel_id=1, source_target_pairs={{0,1},{1,0},{2,3},{3,2},{4,5},{5,4},{6,7},{7,6},{8,9},{9,8},{10,11... | collective-permute-start | bytes 2555912 | tf_op jit(solution)/shard_map/ppermute | solution.py:262
  184.9 9.9 %collective-permute-start.27 = (bf16[1,2,2,2,48,128]{5,4,3,2,1,0:T(8,128)(2,1)}, bf16[1,2,2,2,48,128]{5,4,3,2,1,0:T(8,128)(2,1)}, u32[]{:S(2)}, u32[]{:S(2)}) collective-permute-start(bf16[1,2,2,2,48,128]{5,4,3,2,1,0:T(8,128)(2,1)} %get-tuple-element.282), channel_id=1, source_target_pairs={{0,1},{1,0},{2,3},{3,2},{4,5},{5,4},{6,7},{7,6},{8,9},{9,8},{10,11... | collective-permute-start | bytes 294920 | tf_op jit(solution)/shard_map/ppermute | solution.py:262
  190.4 12.5 %collective-permute-start.13 = (bf16[4,32,1664]{2,1,0:T(8,128)(2,1)}, bf16[4,32,1664]{2,1,0:T(8,128)(2,1)}, u32[]{:S(2)}, u32[]{:S(2)}) collective-permute-start(bf16[4,32,1664]{2,1,0:T(8,128)(2,1)} %get-tuple-element.312), channel_id=1, source_target_pairs={{0,2},{1,3},{2,0},{3,1},{4,6},{5,7},{6,4},{7,5},{8,10},{9,11},{10,... | collective-permute-start | bytes 1277960 | tf_op jit(solution)/shard_map/ppermute | solution.py:262
  199.7 13.5 %collective-permute-start.28 = (bf16[1,16,48,128]{3,2,1,0:T(8,128)(2,1)S(1)}, bf16[1,16,48,128]{3,2,1,0:T(8,128)(2,1)S(1)}, u32[]{:S(2)}, u32[]{:S(2)}) collective-permute-start(bf16[1,16,48,128]{3,2,1,0:T(8,128)(2,1)S(1)} %select_bitcast_fusion.1), channel_id=1, source_target_pairs={{0,16},{16,0},{1,17},{17,1},{2,18},{18,2},{3,19},{19,3},{4,20},{20... | collective-permute-start | bytes 589832 | tf_op jit(solution)/shard_map/ppermute | solution.py:262
  199.7 12.2 %collective-permute-start.36 = (bf16[4,32,1664]{2,1,0:T(8,128)(2,1)}, bf16[4,32,1664]{2,1,0:T(8,128)(2,1)S(1)}, u32[]{:S(2)}, u32[]{:S(2)}) collective-permute-start(bf16[4,32,1664]{2,1,0:T(8,128)(2,1)} %get-tuple-element.313), channel_id=1, source_target_pairs={{0,4},{1,5},{2,6},{3,7},{4,0},{5,1},{6,2},{7,3},{8,12},{9,13},{10,... | collective-permute-start | bytes 1277960 | tf_op jit(solution)/shard_map/ppermute | solution.py:262
  214.2 11.8 %collective-permute-start.37 = (bf16[2,32,1664]{2,1,0:T(8,128)(2,1)S(1)}, bf16[2,32,1664]{2,1,0:T(8,128)(2,1)S(1)}, u32[]{:S(2)}, u32[]{:S(2)}) collective-permute-start(bf16[2,32,1664]{2,1,0:T(8,128)(2,1)S(1)} %get-tuple-element.311), channel_id=1, source_target_pairs={{0,8},{1,9},{2,10},{3,11},{4,12},{5,13},{6,14},{7,15},{8,0},{9,1},... | collective-permute-start | bytes 638984 | tf_op jit(solution)/shard_map/ppermute | solution.py:262
  272.8 11.4 %collective-permute-start.31 = (bf16[4,32,1536]{2,1,0:T(8,128)(2,1)S(1)}, bf16[4,32,1536]{2,1,0:T(8,128)(2,1)S(1)}, u32[]{:S(2)}, u32[]{:S(2)}) collective-permute-start(bf16[4,32,1536]{2,1,0:T(8,128)(2,1)S(1)} %slice.1307), channel_id=1, source_target_pairs={{0,2},{1,3},{2,0},{3,1},{4,6},{5,7},{6,4},{7,5},{8,10},{9,11},{10,... | collective-permute-start | bytes 1179656 | tf_op jit(solution)/shard_map/ppermute | solution.py:262
  274.8 11.6 %collective-permute-start.48 = (bf16[4,32,1536]{2,1,0:T(8,128)(2,1)S(1)}, bf16[4,32,1536]{2,1,0:T(8,128)(2,1)S(1)}, u32[]{:S(2)}, u32[]{:S(2)}) collective-permute-start(bf16[4,32,1536]{2,1,0:T(8,128)(2,1)S(1)} %slice.1306), channel_id=1, source_target_pairs={{0,4},{1,5},{2,6},{3,7},{4,0},{5,1},{6,2},{7,3},{8,12},{9,13},{10,... | collective-permute-start | bytes 1179656 | tf_op jit(solution)/shard_map/ppermute | solution.py:262
  286.5 14.4 %collective-permute-start.49 = (bf16[2,32,1536]{2,1,0:T(8,128)(2,1)S(1)}, bf16[2,32,1536]{2,1,0:T(8,128)(2,1)S(1)}, u32[]{:S(2)}, u32[]{:S(2)}) collective-permute-start(bf16[2,32,1536]{2,1,0:T(8,128)(2,1)S(1)} %slice.1313), channel_id=1, source_target_pairs={{0,8},{1,9},{2,10},{3,11},{4,12},{5,13},{6,14},{7,15},{8,0},{9,1},... | collective-permute-start | bytes 589832 | tf_op jit(solution)/shard_map/ppermute | solution.py:262
  308.3 12.1 %collective-permute-start.52 = (bf16[2,32,1536]{2,1,0:T(8,128)(2,1)S(1)}, bf16[2,32,1536]{2,1,0:T(8,128)(2,1)S(1)}, u32[]{:S(2)}, u32[]{:S(2)}) collective-permute-start(bf16[2,32,1536]{2,1,0:T(8,128)(2,1)S(1)} %pad_maximum_fusion.32), channel_id=1, source_target_pairs={{0,4},{1,5},{2,6},{3,7},{4,0},{5,1},{6,2},{7,3},{8,12},{9,13},{10,... | collective-permute-start | bytes 589832 | tf_op jit(solution)/shard_map/ppermute | solution.py:262
  366.0 16.4 %collective-permute-start.98 = (bf16[2,1,2,2,48,128]{5,4,3,2,1,0:T(8,128)(2,1)S(1)}, bf16[2,1,2,2,48,128]{5,4,3,2,1,0:T(8,128)(2,1)S(1)}, u32[]{:S(2)}, u32[]{:S(2)}) collective-permute-start(bf16[2,1,2,2,48,128]{5,4,3,2,1,0:T(8,128)(2,1)S(1)} %get-tuple-element.276), channel_id=1, source_target_pairs={{0,2},{1,3},{2,0},{3,1},{4,6},{5,7},{6,4},{7,5},{8,10},{9,11},{10,... | collective-permute-start | bytes 294920 | tf_op jit(solution)/shard_map/ppermute | solution.py:262
  380.6 52.2 %collective-permute-start.103 = (bf16[512,1536]{1,0:T(8,128)(2,1)}, bf16[512,1536]{1,0:T(8,128)(2,1)}, u32[]{:S(2)}, u32[]{:S(2)}) collective-permute-start(bf16[512,1536]{1,0:T(8,128)(2,1)} %slice.1292), channel_id=1, source_target_pairs={{0,16},{16,0},{1,17},{17,1},{2,18},{18,2},{3,19},{19,3},{4,20},{20... | collective-permute-start | bytes 4718600 | tf_op jit(solution)/shard_map/ppermute | solution.py:262
  381.9 12.5 %collective-permute-start.73 = (bf16[8,32,1536]{2,1,0:T(8,128)(2,1)}, bf16[8,32,1536]{2,1,0:T(8,128)(2,1)}, u32[]{:S(2)}, u32[]{:S(2)}) collective-permute-start(bf16[8,32,1536]{2,1,0:T(8,128)(2,1)} %bitcast.88), channel_id=1, source_target_pairs={{0,1},{1,0},{2,3},{3,2},{4,5},{5,4},{6,7},{7,6},{8,9},{9,8},{10,11... | collective-permute-start | bytes 2359304 | tf_op jit(solution)/shard_map/ppermute | solution.py:262
  381.9 10.5 %collective-permute-start.55 = (bf16[8,32,1536]{2,1,0:T(8,128)(2,1)}, bf16[8,32,1536]{2,1,0:T(8,128)(2,1)}, u32[]{:S(2)}, u32[]{:S(2)}) collective-permute-start(bf16[8,32,1536]{2,1,0:T(8,128)(2,1)} %bitcast.63), channel_id=1, source_target_pairs={{0,1},{1,0},{2,3},{3,2},{4,5},{5,4},{6,7},{7,6},{8,9},{9,8},{10,11... | collective-permute-start | bytes 2359304 | tf_op jit(solution)/shard_map/ppermute | solution.py:262
  382.4 70.6 %collective-permute-start.102 = (bf16[1536,512]{0,1:T(8,128)(2,1)}, bf16[1536,512]{0,1:T(8,128)(2,1)}, u32[]{:S(2)}, u32[]{:S(2)}) collective-permute-start(bf16[1536,512]{0,1:T(8,128)(2,1)} %slice.1293), channel_id=1, source_target_pairs={{0,16},{16,0},{1,17},{17,1},{2,18},{18,2},{3,19},{19,3},{4,20},{20... | collective-permute-start | bytes 4718600 | tf_op jit(solution)/shard_map/ppermute | solution.py:262
  386.8 96.9 %collective-permute-start.101 = (bf16[1536,512]{0,1:T(8,128)(2,1)}, bf16[1536,512]{0,1:T(8,128)(2,1)}, u32[]{:S(2)}, u32[]{:S(2)}) collective-permute-start(bf16[1536,512]{0,1:T(8,128)(2,1)} %slice.1294), channel_id=1, source_target_pairs={{0,16},{16,0},{1,17},{17,1},{2,18},{18,2},{3,19},{19,3},{4,20},{20... | collective-permute-start | bytes 4718600 | tf_op jit(solution)/shard_map/ppermute | solution.py:262
  393.9 11.0 %collective-permute-start.56 = (bf16[4,32,1536]{2,1,0:T(8,128)(2,1)S(1)}, bf16[4,32,1536]{2,1,0:T(8,128)(2,1)S(1)}, u32[]{:S(2)}, u32[]{:S(2)}) collective-permute-start(bf16[4,32,1536]{2,1,0:T(8,128)(2,1)S(1)} %slice.1305), channel_id=1, source_target_pairs={{0,2},{1,3},{2,0},{3,1},{4,6},{5,7},{6,4},{7,5},{8,10},{9,11},{10,... | collective-permute-start | bytes 1179656 | tf_op jit(solution)/shard_map/ppermute | solution.py:262
  395.8 10.7 %collective-permute-start.74 = (bf16[4,32,1536]{2,1,0:T(8,128)(2,1)S(1)}, bf16[4,32,1536]{2,1,0:T(8,128)(2,1)S(1)}, u32[]{:S(2)}, u32[]{:S(2)}) collective-permute-start(bf16[4,32,1536]{2,1,0:T(8,128)(2,1)S(1)} %slice.1303), channel_id=1, source_target_pairs={{0,4},{1,5},{2,6},{3,7},{4,0},{5,1},{6,2},{7,3},{8,12},{9,13},{10,... | collective-permute-start | bytes 1179656 | tf_op jit(solution)/shard_map/ppermute | solution.py:262
  406.7 14.0 %collective-permute-start.75 = (bf16[2,32,1536]{2,1,0:T(8,128)(2,1)S(1)}, bf16[2,32,1536]{2,1,0:T(8,128)(2,1)S(1)}, u32[]{:S(2)}, u32[]{:S(2)}) collective-permute-start(bf16[2,32,1536]{2,1,0:T(8,128)(2,1)S(1)} %slice.1310), channel_id=1, source_target_pairs={{0,8},{1,9},{2,10},{3,11},{4,12},{5,13},{6,14},{7,15},{8,0},{9,1},... | collective-permute-start | bytes 589832 | tf_op jit(solution)/shard_map/ppermute | solution.py:262
  429.0 65.6 %collective-permute-start.59 = (bf16[1,32,1664]{2,1,0:T(8,128)(2,1)}, bf16[1,32,1664]{2,1,0:T(8,128)(2,1)S(1)}, u32[]{:S(2)}, u32[]{:S(2)}) collective-permute-start(bf16[1,32,1664]{2,1,0:T(8,128)(2,1)} %get-tuple-element.288), channel_id=1, source_target_pairs={{0,8},{1,9},{2,10},{3,11},{4,12},{5,13},{6,14},{7,15},{8,0},{9,1},... | collective-permute-start | bytes 319496 | tf_op jit(solution)/shard_map/ppermute | solution.py:262
  429.7 65.2 %collective-permute-start.77 = (bf16[1,32,1664]{2,1,0:T(8,128)(2,1)}, bf16[1,32,1664]{2,1,0:T(8,128)(2,1)S(1)}, u32[]{:S(2)}, u32[]{:S(2)}) collective-permute-start(bf16[1,32,1664]{2,1,0:T(8,128)(2,1)} %get-tuple-element.290), channel_id=1, source_target_pairs={{0,2},{1,3},{2,0},{3,1},{4,6},{5,7},{6,4},{7,5},{8,10},{9,11},{10,... | collective-permute-start | bytes 319496 | tf_op jit(solution)/shard_map/ppermute | solution.py:262
  495.0 9.9 %collective-permute-start.78 = (bf16[2,32,1664]{2,1,0:T(8,128)(2,1)S(1)}, bf16[2,32,1664]{2,1,0:T(8,128)(2,1)S(1)}, u32[]{:S(2)}, u32[]{:S(2)}) collective-permute-start(bf16[2,32,1664]{2,1,0:T(8,128)(2,1)S(1)} %pad_maximum_fusion.25), channel_id=1, source_target_pairs={{0,8},{1,9},{2,10},{3,11},{4,12},{5,13},{6,14},{7,15},{8,0},{9,1},... | collective-permute-start | bytes 638984 | tf_op jit(solution)/shard_map/ppermute | solution.py:262
  513.5 11.0 %collective-permute-start.80 = (bf16[8,32,1664]{2,1,0:T(8,128)(2,1)S(1)}, bf16[8,32,1664]{2,1,0:T(8,128)(2,1)S(1)}, u32[]{:S(2)}, u32[]{:S(2)}) collective-permute-start(bf16[8,32,1664]{2,1,0:T(8,128)(2,1)S(1)} %pad_maximum_fusion.9), channel_id=1, source_target_pairs={{0,1},{1,0},{2,3},{3,2},{4,5},{5,4},{6,7},{7,6},{8,9},{9,8},{10,11... | collective-permute-start | bytes 2555912 | tf_op jit(solution)/shard_map/ppermute | solution.py:262
  523.2 21.3 %collective-permute-start.63 = (f32[2,256,128]{2,1,0:T(8,128)}, f32[2,256,128]{2,1,0:T(8,128)S(1)}, u32[]{:S(2)}, u32[]{:S(2)}) collective-permute-start(f32[2,256,128]{2,1,0:T(8,128)} %get-tuple-element.55), channel_id=1, source_target_pairs={{16,0},{17,1},{18,2},{19,3},{20,4},{21,5},{22,6},{23,7},{24,8},{25... | collective-permute-start | bytes 786440 | tf_op jit(solution)/shard_map/ppermute | solution.py:24
  534.0 26.8 %collective-permute-start.81 = (f32[2,256,128]{2,1,0:T(8,128)}, f32[2,256,128]{2,1,0:T(8,128)S(1)}, u32[]{:S(2)}, u32[]{:S(2)}) collective-permute-start(f32[2,256,128]{2,1,0:T(8,128)} %get-tuple-element.62), channel_id=1, source_target_pairs={{16,0},{17,1},{18,2},{19,3},{20,4},{21,5},{22,6},{23,7},{24,8},{25... | collective-permute-start | bytes 786440 | tf_op jit(solution)/shard_map/ppermute | solution.py:24
  541.9 79.0 %collective-permute-start.94 = (bf16[192,1536]{1,0:T(8,128)(2,1)}, bf16[192,1536]{1,0:T(8,128)(2,1)}, u32[]{:S(2)}, u32[]{:S(2)}) collective-permute-start(bf16[192,1536]{1,0:T(8,128)(2,1)} %slice.1301), channel_id=1, source_target_pairs={{0,16},{16,0},{1,17},{17,1},{2,18},{18,2},{3,19},{19,3},{4,20},{20... | collective-permute-start | bytes 1769480 | tf_op jit(solution)/shard_map/ppermute | solution.py:262
  579.1 10.6 %collective-permute-start.82 = (f32[2,8,512]{2,1,0:T(8,128)}, f32[2,8,512]{2,1,0:T(8,128)S(1)}, u32[]{:S(2)}, u32[]{:S(2)}) collective-permute-start(f32[2,8,512]{2,1,0:T(8,128)} %get-tuple-element.65), channel_id=1, source_target_pairs={{16,0},{17,1},{18,2},{19,3},{20,4},{21,5},{22,6},{23,7},{24,8},{25... | collective-permute-start | bytes 98312 | tf_op jit(solution)/shard_map/ppermute | solution.py:24
  608.9 14.7 %collective-permute-start.83 = (bf16[8,32,1536]{2,1,0:T(8,128)(2,1)}, bf16[8,32,1536]{2,1,0:T(8,128)(2,1)}, u32[]{:S(2)}, u32[]{:S(2)}) collective-permute-start(bf16[8,32,1536]{2,1,0:T(8,128)(2,1)} %bitcast.359), channel_id=1, source_target_pairs={{0,1},{1,0},{2,3},{3,2},{4,5},{5,4},{6,7},{7,6},{8,9},{9,8},{10,11... | collective-permute-start | bytes 2359304 | tf_op jit(solution)/shard_map/ppermute | solution.py:262
  609.0 16.7 %collective-permute-start.65 = (bf16[8,32,1536]{2,1,0:T(8,128)(2,1)}, bf16[8,32,1536]{2,1,0:T(8,128)(2,1)}, u32[]{:S(2)}, u32[]{:S(2)}) collective-permute-start(bf16[8,32,1536]{2,1,0:T(8,128)(2,1)} %bitcast.358), channel_id=1, source_target_pairs={{0,1},{1,0},{2,3},{3,2},{4,5},{5,4},{6,7},{7,6},{8,9},{9,8},{10,11... | collective-permute-start | bytes 2359304 | tf_op jit(solution)/shard_map/ppermute | solution.py:262
  610.6 58.1 %collective-permute-start.92 = (bf16[1536,387]{0,1:T(8,128)(2,1)}, bf16[1536,387]{0,1:T(8,128)(2,1)}, u32[]{:S(2)}, u32[]{:S(2)}) collective-permute-start(bf16[1536,387]{0,1:T(8,128)(2,1)} %pad_maximum_fusion.7), channel_id=1, source_target_pairs={{0,16},{16,0},{1,17},{17,1},{2,18},{18,2},{3,19},{19,3},{4,20},{20... | collective-permute-start | bytes 3566600 | tf_op jit(solution)/shard_map/ppermute | solution.py:262
  620.5 37.1 %collective-permute-start.87 = (f32[1,16,104,128]{3,2,1,0:T(8,128)S(1)}, f32[1,16,104,128]{3,2,1,0:T(8,128)S(1)}, u32[]{:S(2)}, u32[]{:S(2)}) collective-permute-start(f32[1,16,104,128]{3,2,1,0:T(8,128)S(1)} %slice.923), channel_id=1, source_target_pairs={{0,16},{16,0},{1,17},{17,1},{2,18},{18,2},{3,19},{19,3},{4,20},{20... | collective-permute-start | bytes 2555912 | tf_op jit(solution)/shard_map/ppermute | solution.py:262
  625.1 37.6 %collective-permute-start.84 = (bf16[4,32,1536]{2,1,0:T(8,128)(2,1)S(1)}, bf16[4,32,1536]{2,1,0:T(8,128)(2,1)}, u32[]{:S(2)}, u32[]{:S(2)}) collective-permute-start(bf16[4,32,1536]{2,1,0:T(8,128)(2,1)S(1)} %slice.1302), channel_id=1, source_target_pairs={{0,4},{1,5},{2,6},{3,7},{4,0},{5,1},{6,2},{7,3},{8,12},{9,13},{10,... | collective-permute-start | bytes 1179656 | tf_op jit(solution)/shard_map/ppermute | solution.py:262
  627.8 37.3 %collective-permute-start.66 = (bf16[4,32,1536]{2,1,0:T(8,128)(2,1)}, bf16[4,32,1536]{2,1,0:T(8,128)(2,1)}, u32[]{:S(2)}, u32[]{:S(2)}) collective-permute-start(bf16[4,32,1536]{2,1,0:T(8,128)(2,1)} %slice.1304), channel_id=1, source_target_pairs={{0,2},{1,3},{2,0},{3,1},{4,6},{5,7},{6,4},{7,5},{8,10},{9,11},{10,... | collective-permute-start | bytes 1179656 | tf_op jit(solution)/shard_map/ppermute | solution.py:262
  662.6 9.9 %collective-permute-start.88 = (f32[8,104,128]{2,1,0:T(8,128)S(1)}, f32[8,104,128]{2,1,0:T(8,128)S(1)}, u32[]{:S(2)}, u32[]{:S(2)}) collective-permute-start(f32[8,104,128]{2,1,0:T(8,128)S(1)} %slice.925), channel_id=1, source_target_pairs={{0,1},{1,0},{2,3},{3,2},{4,5},{5,4},{6,7},{7,6},{8,9},{9,8},{10,11... | collective-permute-start | bytes 1277960 | tf_op jit(solution)/shard_map/ppermute | solution.py:262
  663.8 12.6 %collective-permute-start.85 = (bf16[2,32,1536]{2,1,0:T(8,128)(2,1)S(1)}, bf16[2,32,1536]{2,1,0:T(8,128)(2,1)S(1)}, u32[]{:S(2)}, u32[]{:S(2)}) collective-permute-start(bf16[2,32,1536]{2,1,0:T(8,128)(2,1)S(1)} %slice.1309), channel_id=1, source_target_pairs={{0,8},{1,9},{2,10},{3,11},{4,12},{5,13},{6,14},{7,15},{8,0},{9,1},... | collective-permute-start | bytes 589832 | tf_op jit(solution)/shard_map/ppermute | solution.py:262
  666.2 11.5 %collective-permute-start.67 = (bf16[2,32,1536]{2,1,0:T(8,128)(2,1)S(1)}, bf16[2,32,1536]{2,1,0:T(8,128)(2,1)S(1)}, u32[]{:S(2)}, u32[]{:S(2)}) collective-permute-start(bf16[2,32,1536]{2,1,0:T(8,128)(2,1)S(1)} %slice.1311), channel_id=1, source_target_pairs={{0,4},{1,5},{2,6},{3,7},{4,0},{5,1},{6,2},{7,3},{8,12},{9,13},{10,... | collective-permute-start | bytes 589832 | tf_op jit(solution)/shard_map/ppermute | solution.py:262
  672.6 13.5 %collective-permute-start.89 = (f32[4,104,128]{2,1,0:T(8,128)S(1)}, f32[4,104,128]{2,1,0:T(8,128)S(1)}, u32[]{:S(2)}, u32[]{:S(2)}) collective-permute-start(f32[4,104,128]{2,1,0:T(8,128)S(1)} %slice.927), channel_id=1, source_target_pairs={{0,2},{1,3},{2,0},{3,1},{4,6},{5,7},{6,4},{7,5},{8,10},{9,11},{10,... | collective-permute-start | bytes 638984 | tf_op jit(solution)/shard_map/ppermute | solution.py:262
  (224 other events, 1733.4 us)
